TPU v7x, 32 devices: a whole 2x2x4 slice. The times are simulated.
32 devices in a mesh: seq: 32 (over z, y, x, core), ch: 1.
Axes of the slice: x: 2, y: 2, z: 4, core: 2. Of those that a mesh axis runs over, the one named last changes fastest.
Arguments:
- q_feat: bfloat16 [8192, 4096], P('seq', 'ch'), may hold values from -6 to 6
- k_feat: bfloat16 [8192, 4096], P('seq', 'ch'), may hold values from -6 to 6
- v_feat: bfloat16 [8192, 4096], P('seq', 'ch'), may hold values from -6 to 6
- short_taps: float32 [3, 3, 4096], P(None, None, 'ch'), may hold values from -3.5 to 3.5
- decay_rate: float32 [16, 4096], P(None, 'ch'), may hold values from 0 to 1, as said below
- residue: float32 [16, 4096], P(None, 'ch'), may hold values from -1 to 1
- skip_gain: float32 [4096], P('ch'), may hold values from -6 to 6
- out_weight: bfloat16 [4096, 4096], P('seq', 'ch'), may hold values from -0.09375 to 0.09375
- doc_starts: int32 [32, 4], P('seq'), may hold values from 0 to 256, as said below
- reset_flags: int32 [32, 4], P('seq'), may hold values from 0 to 1, as said below
Outputs:
- mixer_out: bfloat16 [8192, 4096], P('seq', 'ch')
Inputs may be any that keep to these rules, and one draw needn't show every extreme that they name: `doc_starts`: row s lists ascending the offsets within shard s at which documents begin, then unused slots holding 256; a shard holds at most 4 starts, some shard exactly 4, some shard none. `reset_flags`: only used slots hold 1; in each shard at most one slot holds 1, and some shard has one. `decay_rate`: positive rates.
All inputs are finite; a program needn't handle non-finite values.
Results may differ from a plain program's by a relative error of at most 0.018.
Values may be sent and summed in bfloat16 or wider, within the bound.
A program may use at most 256 MiB of HBM per device.

v0:
```python
import math

import jax
import jax.numpy as jnp
from jax import lax
from jax.sharding import PartitionSpec as P

BLOCK = 128


def from_behind(block, axis, distance):
    devices = range(lax.axis_size(axis))
    route = [(i - distance, i) for i in devices if i - distance in devices]
    return lax.ppermute(block, axis, route)


def entering_2(value, axis, join, neutral):
    count, mine = (lax.axis_size(axis), lax.axis_index(axis))
    pieces = jax.tree.map(lambda part: lax.all_gather(part, axis), value)
    running = jax.tree.map(
        lambda part, zero: jnp.full_like(part, 0) + jnp.asarray(zero, part.dtype), value, neutral
    )

    def hop(position, running):
        longer = join(running, jax.tree.map(lambda part: part[position], pieces))
        return jax.tree.map(lambda new, old: jnp.where(position < mine, new, old), longer, running)

    return lax.fori_loop(0, count - 1, hop, running)


def short_filter(features, rim_rows, tap_weights, keep_mask):
    token_rows = features.shape[0]
    tap_count = tap_weights.shape[0]
    joined = jnp.concatenate([rim_rows, features], axis=0)
    summed = tap_weights[0] * features.astype(jnp.float32)
    valid_mask = jnp.ones((token_rows,), jnp.float32)
    for offset in range(1, tap_count):
        valid_mask = valid_mask * jnp.concatenate(
            [jnp.ones((offset - 1,), jnp.float32), keep_mask[: token_rows - offset + 1]]
        )
        lagged = joined[tap_count - 1 - offset : tap_count - 1 - offset + token_rows].astype(
            jnp.float32
        )
        summed = summed + tap_weights[offset] * valid_mask[:, None] * lagged
    return summed.astype(jnp.bfloat16)


def transform_tables(length):
    period = 2 * length
    time_axis = jnp.arange(length, dtype=jnp.int32)
    cos_freq = jnp.arange(length + 1, dtype=jnp.int32)
    sin_freq = jnp.arange(1, length, dtype=jnp.int32)
    cos_angle = (
        2.0
        * math.pi
        / period
        * (cos_freq[:, None] * time_axis[None, :] % period).astype(jnp.float32)
    )
    sin_angle = (
        2.0
        * math.pi
        / period
        * (sin_freq[:, None] * time_axis[None, :] % period).astype(jnp.float32)
    )
    forward = jnp.concatenate([jnp.cos(cos_angle), jnp.sin(sin_angle)], axis=0)
    edge_weight = (
        jnp.where((cos_freq == 0) | (cos_freq == length), 1.0, 2.0).astype(jnp.float32) / period
    )
    inverse = jnp.concatenate(
        [(jnp.cos(cos_angle) * edge_weight[:, None]).T, (jnp.sin(sin_angle) * (2.0 / period)).T],
        axis=1,
    )
    return (forward, inverse)


def chain_combine(earlier, later):
    return (earlier[0] * later[0], later[0] * earlier[1] + later[1])


def local(
    q_feat,
    k_feat,
    v_feat,
    short_taps,
    decay_rate,
    residue,
    skip_gain,
    out_weight,
    doc_starts,
    reset_flags,
):
    highest = lax.Precision.HIGHEST
    token_rows, channels = q_feat.shape
    tap_count = short_taps.shape[1]
    block_count = token_rows // BLOCK
    position = jnp.arange(token_rows, dtype=jnp.int32)
    matches = position[:, None] == doc_starts[0][None, :]
    starts_here = jnp.any(matches, axis=1).astype(jnp.float32)
    resets = jnp.any(matches & (reset_flags[0][None, :] == 1), axis=1).astype(jnp.float32)
    keep_mask = 1.0 - starts_here
    rim_keep = []
    for offset in range(tap_count - 1):
        rim_index = token_rows - (tap_count - 1) + offset
        rim_keep.append(jnp.prod(keep_mask[rim_index + 1 :]))
    rim_scale = jnp.stack(rim_keep).astype(jnp.bfloat16)
    three_feats = (q_feat, k_feat, v_feat)
    tails = (
        jnp.stack([feature_rows[token_rows - (tap_count - 1) :] for feature_rows in three_feats])
        * rim_scale[None, :, None]
    )
    arrived = from_behind(tails, "seq", 1)
    q_short = short_filter(q_feat, arrived[0], short_taps[0], keep_mask)
    k_short = short_filter(k_feat, arrived[1], short_taps[1], keep_mask)
    v_short = short_filter(v_feat, arrived[2], short_taps[2], keep_mask)
    gated = k_short.astype(jnp.float32) * v_short.astype(jnp.float32)
    forward, inverse = transform_tables(BLOCK)
    steps_axis = jnp.arange(BLOCK + 1, dtype=jnp.float32)
    powers = jnp.exp(-steps_axis[None, :, None] * decay_rate[:, None, :])
    filter_taps = jnp.einsum("njc,nc->jc", powers[:, :BLOCK], residue, precision=highest)
    spectrum = jnp.dot(forward, filter_taps, precision=highest)
    cos_part = spectrum[: BLOCK + 1]
    sin_part = spectrum[BLOCK + 1 :]
    reset_blocks = resets.reshape(block_count, BLOCK)
    block_pos = jnp.arange(BLOCK, dtype=jnp.float32)
    has_reset = jnp.sum(reset_blocks, axis=1)
    cut_index = jnp.sum(reset_blocks * block_pos[None, :], axis=1)
    after_cut = (block_pos[None, :] >= cut_index[:, None]).astype(jnp.float32)
    blocks = gated.reshape(block_count, BLOCK, channels)
    late_part = blocks * after_cut[:, :, None]
    freq_data = jnp.einsum("fs,bsc->bfc", forward, blocks, precision=highest)
    data_cos = freq_data[:, : BLOCK + 1]
    data_sin = freq_data[:, BLOCK + 1 :]
    cross_term = data_sin * sin_part[None]
    edge_rows = jnp.zeros((block_count, 1, channels), jnp.float32)
    real_part = data_cos * cos_part[None] - jnp.concatenate(
        [edge_rows, cross_term, edge_rows], axis=1
    )
    imag_part = data_cos[:, 1:BLOCK] * sin_part[None] + data_sin * cos_part[None, 1:BLOCK]
    outputs = jnp.einsum(
        "tf,bfc->btc", inverse, jnp.concatenate([real_part, imag_part], axis=1), precision=highest
    )
    block_ids = jnp.arange(block_count, dtype=jnp.float32)
    reset_block = jnp.sum(has_reset * block_ids).astype(jnp.int32)
    cut_here = lax.dynamic_index_in_dim(cut_index, reset_block, 0, keepdims=False)
    flag_here = lax.dynamic_index_in_dim(has_reset, reset_block, 0, keepdims=False)
    early_rows = lax.dynamic_index_in_dim(blocks, reset_block, 0, keepdims=False)
    early_mask = (block_pos < cut_here).astype(jnp.float32)
    early_lag = jnp.maximum(cut_here - 1.0 - block_pos, 0.0)
    early_weight = jnp.exp(-early_lag[:, None, None] * decay_rate[None]) * early_mask[:, None, None]
    early_state = jnp.einsum("snc,sc->nc", early_weight, early_rows, precision=highest)
    late_gap = jnp.maximum(block_pos - cut_here + 1.0, 0.0)
    late_weight = jnp.exp(-late_gap[:, None, None] * decay_rate[None]) * residue[None]
    leaked = (
        jnp.einsum("tnc,nc->tc", late_weight, early_state, precision=highest)
        * ((1.0 - early_mask) * flag_here)[:, None]
    )
    current = lax.dynamic_index_in_dim(outputs, reset_block, 0, keepdims=True)
    within = lax.dynamic_update_slice_in_dim(outputs, current - leaked[None], reset_block, 0)
    reversed_powers = powers[:, BLOCK - 1 :: -1]
    block_states = jnp.einsum("nsc,bsc->bnc", reversed_powers, late_part, precision=highest)
    block_pass = powers[None, :, BLOCK] * (1.0 - has_reset)[:, None, None]

    def advance(carried_state, block_item):
        pass_factor, fresh_state = block_item
        product_pass, summed_state = carried_state
        return (
            (product_pass * pass_factor, pass_factor * summed_state + fresh_state),
            (product_pass, summed_state),
        )

    starting = (jnp.ones_like(decay_rate), jnp.zeros_like(decay_rate))
    (shard_pass, shard_state), (lead_pass, lead_state) = lax.scan(
        advance, starting, (block_pass, block_states)
    )
    _, entering = entering_2(
        (shard_pass, shard_state),
        "seq",
        chain_combine,
        (jnp.ones_like(shard_pass), jnp.zeros_like(shard_state)),
    )
    entering_states = lead_pass * entering[None] + lead_state
    alive_mask = 1.0 - has_reset[:, None] * after_cut
    weighted = residue[:, None, :] * powers[:, 1:]
    carried = (
        jnp.einsum("nic,bnc->bic", weighted, entering_states, precision=highest)
        * alive_mask[:, :, None]
    )
    filtered = (within + carried).reshape(token_rows, channels)
    mixed = (q_short.astype(jnp.float32) * (filtered + skip_gain[None, :] * gated)).astype(
        jnp.bfloat16
    )
    projected = lax.dot_general(
        mixed,
        lax.all_gather(out_weight, "seq", axis=0, tiled=True),
        (((1,), (1,)), ((), ())),
        preferred_element_type=jnp.float32,
    )
    result = lax.psum_scatter(projected.astype(jnp.bfloat16), "ch", scatter_dimension=1, tiled=True)
    return result


def solution(mesh):
    placed = (
        P("seq", "ch"),
        P("seq", "ch"),
        P("seq", "ch"),
        P(None, None, "ch"),
        P(None, "ch"),
        P(None, "ch"),
        P("ch"),
        P("seq", "ch"),
        P("seq", None),
        P("seq", None),
    )
    return jax.shard_map(
        local, mesh=mesh, in_specs=placed, out_specs=P("seq", "ch"), check_vma=False
    )
```

profile of v0, /device:TPU:0, one launch (start us, length us, event | category | flops | bytes accessed | tf_op | source)
XLA Modules:
  0.0 592.9 jit_solution(8661420900340378933)
XLA Ops:
  11.8 3.0 collective-permute-start
  17.5 6.3 %multiply_exponential_fusion = f32[16,129,4096]{2,0,1:T(8,128)S(1)} fusion(f32[16,4096]{1,0:T(8,128)} %param.18, f32[129]{0:T(256)S(1)} %iota_negate_fusion), kind=kLoop, calls=%fused_computation.8 | loop fusion | flops 8454144 | bytes 34079236 | tf_op jit(solution)/shard_map/exp | solution.py:118
  23.8 11.1 %copy-done = f32[16,129,4096]{2,0,1:T(8,128)} copy-done((f32[16,129,4096]{2,0,1:T(8,128)}, f32[16,129,4096]{2,0,1:T(8,128)S(1)}, u32[]{:S(2)}) %copy-start) | copy-done | bytes 33816600
  35.0 44.2 %slice_multiply_fusion = (f32[16,128,4096]{2,0,1:T(8,128)}, f32[16,128,4096]{2,0,1:T(8,128)}) fusion(f32[16,129,4096]{2,0,1:T(8,128)} %copy-done, f32[16,4096]{1,0:T(8,128)S(1)} %copy-done.10), kind=kLoop, calls=%fused_computation.9 | loop fusion | flops 8388608 | bytes 134479872 | tf_op jit(solution)/shard_map/mul | solution.py:183
  79.9 22.8 %rev.3 = f32[16,128,4096]{2,0,1:T(8,128)} reverse(f32[16,128,4096]{2,0,1:T(8,128)} %get-tuple-element.240), dimensions={1} | reverse | bytes 67108864 | tf_op jit(solution)/shard_map/rev | solution.py:159
  102.8 33.7 %copy.25 = f32[16,128,4096]{1,0,2:T(8,128)} copy(f32[16,128,4096]{2,0,1:T(8,128)} %rev.3) | data formatting | bytes 67108864 | tf_op jit(solution)/shard_map/rev | solution.py:159
  137.3 7.8 %convert_multiply_fusion = f32[256,4096]{1,0:T(8,128)} fusion(bf16[256,4096]{1,0:T(8,128)(2,1)S(1)} %copy-done.8, bf16[2,4096]{1,0:T(2,128)(2,1)S(1)} %get-tuple-element.256, bf16[256,4096]{1,0:T(8,128)(2,1)} %param.16, bf16[2,4096]{1,0:T(2,128)(2,1)S(1)} %get-tuple-element.255, f32[4096]{0:T(1024)S(1)} %bitcast.132, f32[4096]{0:T(1024)S(1)} %bitcast.133, ...), kind=kLoop, calls=%fused_computation.29 | loop fusion | flops 38797312 | bytes 8521728 | tf_op jit(solution)/shard_map/mul | solution.py:115
  145.1 7.2 %copy.24 = f32[2,128,4096]{1,0,2:T(2,128)} copy(f32[2,128,4096]{2,1,0:T(8,128)} %bitcast.118) | data formatting | bytes 8388608 | tf_op jit(solution)/shard_map/reshape | solution.py:128
  152.3 56.7 %fusion.11 = f32[2,16,4096]{1,0,2:T(2,128)} fusion(f32[16,128,4096]{1,0,2:T(8,128)} %copy.25, f32[2,128,4096]{1,0,2:T(2,128)} %copy.24, f32[2,128]{1,0:T(2,128)S(1)} %copy-done.18), kind=kOutput, calls=%fused_computation.34 | convolution fusion | flops 202375168 | bytes 38274048 | tf_op jit(solution)/shard_map/nsc,bsc->bnc/dot_general | solution.py:160
  209.0 5.2 copy.26
  214.2 2.0 while.31
  220.8 15.5 %multiply_reduce_fusion.2 = f32[4096,128]{0,1:T(8,128)S(1)} fusion(f32[4096,16]{0,1:T(8,128)S(1)} %bitcast.122, f32[16,129,4096]{2,0,1:T(8,128)} %copy-done), kind=kLoop, calls=%fused_computation.12 | loop fusion | flops 16252928 | bytes 35913728 | tf_op jit(solution)/shard_map/njc,nc->jc/dot_general | solution.py:119
  236.4 3.6 fusion.30
  240.0 2.0 copy-done.5
  242.0 33.6 %copy.28 = f32[16,128,4096]{1,0,2:T(8,128)} copy(f32[16,128,4096]{2,0,1:T(8,128)} %get-tuple-element.239) | data formatting | bytes 67108864 | tf_op jit(solution)/shard_map/mul | solution.py:183
  279.0 4.1 fusion.64
  283.1 9.1 %convolution_bitcast_fusion = f32[2,256,4096]{2,1,0:T(8,128)} fusion(f32[2,128,4096]{2,1,0:T(8,128)S(1)} %bitcast.119, f32[127,128]{1,0:T(8,128)S(1)} %fusion.41, f32[129,128]{1,0:T(8,128)S(1)} %fusion.34), kind=kOutput, calls=%fused_computation.17 | convolution fusion | flops 3221258240 | bytes 12713984 | tf_op jit(solution)/shard_map/fs,bsc->bfc/dot_general | solution.py:130
  292.2 10.0 %slice_multiply_fusion.3 = (f32[2,127,4096]{2,1,0:T(8,128)}, f32[2,127,4096]{2,1,0:T(8,128)}) fusion(f32[2,256,4096]{2,1,0:T(8,128)} %convolution_bitcast_fusion, f32[127,4096]{1,0:T(8,128)S(1)} %get-tuple-element.243, f32[127,4096]{1,0:T(8,128)} %get-tuple-element.244), kind=kLoop, calls=%fused_computation.33 | loop fusion | flops 4161536 | bytes 20807680 | tf_op jit(solution)/shard_map/mul | solution.py:133
  302.3 4.6 fusion.5
  307.2 5.7 fusion.1
  317.2 7.3 %multiply_reduce_fusion.1 = f32[4096,16]{0,1:T(8,128)S(1)} fusion(f32[4096,128]{0,1:T(8,128)S(1)} %dynamic-slice_bitcast_fusion, f32[128]{0:T(128)S(1)} %compare_convert_fusion, f32[16,4096]{1,0:T(8,128)S(1)} %copy-done.13, f32[128]{0:T(128)S(1)} %maximum_negate_fusion.1), kind=kLoop, calls=%fused_computation.11 | loop fusion | flops 33488896 | bytes 2622464 | tf_op jit(solution)/shard_map/snc,sc->nc/dot_general | solution.py:150
  324.4 11.6 %multiply_reduce_fusion = f32[4096,128]{0,1:T(8,128)S(1)} fusion(f32[4096,16]{0,1:T(8,128)S(1)} %multiply_reduce_fusion.1, f32[16,4096]{1,0:T(8,128)S(1)} %copy-done.10, f32[128]{0:T(128)S(1)} %get-tuple-element.264, f32[16,4096]{1,0:T(8,128)S(1)} %copy-done.13), kind=kLoop, calls=%fused_computation.10 | loop fusion | flops 33030144 | bytes 2884096 | tf_op jit(solution)/shard_map/tnc,nc->tc/dot_general | solution.py:154
  336.3 3.4 fusion.17
  339.6 35.0 %all-gather.10.cloned.1.call-done = f32[512,4096]{1,0:T(8,128)} async-done(((f32[16,4096]{1,0:T(8,128)}), f32[512,4096]{1,0:T(8,128)}) %all-gather.10.cloned.1.call-update) | async-done | bytes 8388624 | tf_op jit(solution)/shard_map/all_gather | solution.py:19
  374.7 39.7 %while.32 = (s32[]{:T(128)}, f32[16,4096]{1,0:T(8,128)S(1)}, s32[]{:T(128)}, f32[32,16,4096]{2,1,0:T(8,128)}, f32[32,16,4096]{2,1,0:T(8,128)}, /*index=5*/s32[]{:T(128)}, s32[]{:T(128)}) while((s32[]{:T(128)}, f32[16,4096]{1,0:T(8,128)S(1)}, s32[]{:T(128)}, f32[32,16,4096]{2,1,0:T(8,128)}, f32[32,16,4096]{2,1,0:T(8,128)}, ...), condition=%wide.region_8.9_spmd.clone, body=%wide.region_7.8_spmd.clone.sunk | while | flops 262148 | bytes 1048685 | solution.py:28
  414.5 4.4 copy.27
  418.9 33.1 %fusion.66 = f32[4096,2,128]{2,1,0:T(2,128)} fusion(f32[2,16,4096]{1,0,2:T(2,128)} %copy.27, f32[16,128,4096]{1,0,2:T(8,128)} %copy.28), kind=kOutput, calls=%fused_computation.140 | convolution fusion | flops 201326592 | bytes 38273024 | tf_op jit(solution)/shard_map/nic,bnc->bic/dot_general | solution.py:185
  452.0 7.3 %copy.29 = f32[4096,2,128]{0,2,1:T(8,128)} copy(f32[4096,2,128]{2,1,0:T(2,128)} %fusion.66) | data formatting | bytes 8388608 | tf_op jit(solution)/shard_map/nic,bnc->bic/dot_general | solution.py:185
  459.4 4.4 bitcast_add_fusion.3
  464.7 3.0 fusion.8
  467.7 102.7 %all-gather.6.cloned.1.call-done = bf16[4096,4096]{1,0:T(8,128)(2,1)} async-done(((bf16[128,4096]{1,0:T(8,128)(2,1)}), bf16[4096,4096]{1,0:T(8,128)(2,1)}) %all-gather.6.cloned.1.call-update) | async-done | bytes 33554448 | tf_op jit(solution)/shard_map/all_gather | solution.py:194
  570.4 15.7 %convolution_convert_fusion = bf16[256,4096]{1,0:T(8,128)(2,1)} fusion(bf16[256,4096]{1,0:T(8,128)(2,1)S(1)} %fusion.8, bf16[4096,4096]{1,0:T(8,128)(2,1)} %all-gather.6.cloned.1.call-done), kind=kOutput, calls=%fused_computation.18 | convolution fusion | flops 8590983168 | bytes 37748736 | tf_op jit(solution)/shard_map/dot_general | solution.py:192
  (133 shorter events, 62.7 us)
Async XLA Ops:
  6.5 333.1 %all-gather.8.cloned.1.call-start = ((), (), s32[]{:S(2)}) async-start(), calls=%async_computation.1 | async-start | bytes 8650752 | tf_op jit(solution)/shard_map/all_gather | solution.py:19
  8.8 0.7 copy-start.19
  11.8 124.7 %collective-permute-start = (bf16[3,2,4096]{2,1,0:T(2,128)(2,1)S(1)}, bf16[3,2,4096]{2,1,0:T(2,128)(2,1)}, u32[]{:S(2)}, u32[]{:S(2)}) collective-permute-start(bf16[3,2,4096]{2,1,0:T(2,128)(2,1)S(1)} %maximum_multiply_fusion), channel_id=1, source_target_pairs={{0,1},{1,2},{2,3},{3,4},{4,5},{5,6},{6,7},{7,8},{8,9},{9,10},{10,1... | collective-permute-start | bytes 147464 | tf_op jit(solution)/shard_map/ppermute | solution.py:14
  16.9 6.9 %copy-start.24 = (f32[2]{0:T(128)}, f32[2]{0:T(128)S(1)}, u32[]{:S(2)}) copy-start(f32[2]{0:T(128)S(1)} %get-tuple-element.208) | copy-start | bytes 28
  16.9 62.4 %copy-start.22 = (f32[2]{0:T(128)}, f32[2]{0:T(128)S(1)}, u32[]{:S(2)}) copy-start(f32[2]{0:T(128)S(1)} %get-tuple-element.207) | copy-start | bytes 28
  17.5 17.5 %copy-start.10 = (f32[16,4096]{1,0:T(8,128)S(1)}, f32[16,4096]{1,0:T(8,128)}, u32[]{:S(2)}) copy-start(f32[16,4096]{1,0:T(8,128)} %param.19) | copy-start | bytes 786436
  23.8 11.1 %copy-start = (f32[16,129,4096]{2,0,1:T(8,128)}, f32[16,129,4096]{2,0,1:T(8,128)S(1)}, u32[]{:S(2)}) copy-start(f32[16,129,4096]{2,0,1:T(8,128)S(1)} %multiply_exponential_fusion) | copy-start | bytes 101449728
  102.8 34.5 %copy-start.8 = (bf16[256,4096]{1,0:T(8,128)(2,1)S(1)}, bf16[256,4096]{1,0:T(8,128)(2,1)}, u32[]{:S(2)}) copy-start(bf16[256,4096]{1,0:T(8,128)(2,1)} %param.15) | copy-start | bytes 6291460
  145.1 7.2 %copy-start.18 = (f32[2,128]{1,0:T(2,128)S(1)}, f32[2,128]{1,0:T(2,128)}, u32[]{:S(2)}) copy-start(f32[2,128]{1,0:T(2,128)} %fusion.59) | copy-start | bytes 3076
  214.2 4.9 copy-start.23
  214.2 5.5 copy-start.25
  216.2 0.7 copy-start.3
  216.3 0.8 copy-start.4
  217.0 157.7 %all-gather.10.cloned.1.call-start = ((), (), s32[]{:S(2)}) async-start(), calls=%async_computation.2 | async-start | bytes 8650752 | tf_op jit(solution)/shard_map/all_gather | solution.py:19
  217.7 352.6 %all-gather.6.cloned.1.call-start = ((), (), s32[]{:S(2)}) async-start(), calls=%async_computation | async-start | bytes 34603008 | tf_op jit(solution)/shard_map/all_gather | solution.py:194
  240.0 2.0 copy-start.5
  279.0 4.1 copy-start.1
  292.2 10.1 %slice-start = ((f32[256,4096]{1,0:T(8,128)}), f32[129,4096]{1,0:T(8,128)S(1)}, s32[]{:S(2)}) async-start(f32[256,4096]{1,0:T(8,128)} %copy-done.5), calls=%async_computation.3 | async-start | bytes 4456448 | tf_op jit(solution)/shard_map/slice | solution.py:121
  302.2 4.9 copy-start.7
  312.9 3.3 copy-start.6
  316.2 0.9 copy-start.13
  339.6 74.8 %copy-start.11 = (f32[2,16,4096]{2,1,0:T(8,128)S(1)}, f32[2,16,4096]{2,1,0:T(8,128)}, u32[]{:S(2)}) copy-start(f32[2,16,4096]{2,1,0:T(8,128)} %get-tuple-element.139) | copy-start | bytes 1572868
  339.6 74.8 %copy-start.12 = (f32[2,16,4096]{2,1,0:T(8,128)S(1)}, f32[2,16,4096]{2,1,0:T(8,128)}, u32[]{:S(2)}) copy-start(f32[2,16,4096]{2,1,0:T(8,128)} %get-tuple-element.143) | copy-start | bytes 1572868
  459.3 4.6 copy-start.2
  459.3 5.3 copy-start.9
  459.3 5.3 copy-start.14
  459.3 5.3 copy-start.15
  459.3 5.3 copy-start.16
  459.3 5.3 copy-start.17
  459.3 5.3 copy-start.20
  459.4 5.3 copy-start.21
Sparse Core Ops, SparseCore 0:
  217.1 78.9 all-gather.7
  299.0 75.6 all-gather.9
  377.6 192.7 all-gather.5
where the time goes:
time: 599 us; the launch traced here: 593 us
  other arithmetic  167 us (28%)
  local copies, waits for them, and re-layouts  144 us (24%)
  waiting for transfers between devices  139 us (23%)
  matrix products  124 us (21%)
  between operations  15.2 us (3%)
    all_gather x1, waiting for transfers between devices, local(): lax.all_gather(out_weight, 'seq', axis=0, tiled=True)  103 us
    dot_general x1, matrix products, local(): jnp.einsum('nsc,bsc->bnc', reversed_powers, late_part, precision=highest)  56.7 us
    rev x2, local copies, waits for them, and re-layouts, local(): reversed_powers = powers[:, BLOCK - 1::-1]  56.6 us
    mul x1, other arithmetic, local(): weighted = residue[:, None, :] * powers[:, 1:]  44.2 us
    select_n x31, other arithmetic, hop(): jnp.where(position < mine, new, old)  39 us
    all_gather x2, waiting for transfers between devices, entering_2(): pieces = jax.tree.map(lambda part: lax.all_gather(part, axis), value)  35 us
    mul x1, local copies, waits for them, and re-layouts, local(): weighted = residue[:, None, :] * powers[:, 1:]  33.6 us
    dot_general x1, matrix products, local(): jnp.einsum('nic,bnc->bic', weighted, entering_states, precision=highest)  33.1 us
  transfers between devices with their start and end apart: 4, of which 2 were waited for; matrix products, arithmetic and copies ran while one was open for 53% of the time, Pallas kernels for 0%

commit v1 on v0

v1 whole, which is shorter than its diff:
```python
import functools

import jax
import jax.numpy as jnp
from jax import lax
from jax.experimental import pallas as pl
from jax.experimental.pallas import tpu as pltpu
from jax.sharding import PartitionSpec as P

LANES = 128
GROUPS = 8
TILE = LANES * GROUPS
ROWS = 16
UNROLL = 8


def cut_of(starts, flags, tokens):
    cut = jnp.int32(tokens)
    for slot in range(starts.shape[1]):
        cut = jnp.where(flags[0, slot] == 1, jnp.minimum(cut, starts[0, slot]), cut)
    return cut


def local_kernel(starts, flags, q_ref, k_ref, v_ref, rim_ref, taps_ref, rate_ref, res_ref,
                 skip_ref, qs_ref, z_ref, state_ref, fac_ref):
    tokens = q_ref.shape[0]
    modes = rate_ref.shape[0]
    slots = starts.shape[1]
    cut = cut_of(starts, flags, tokens)

    def short_rows(step, carry):
        row = pl.multiple_of(step * ROWS, ROWS)
        back = pl.multiple_of(jnp.maximum(row - ROWS, 0), ROWS)
        at = lax.broadcasted_iota(jnp.int32, (ROWS, LANES), 0) + row
        hit = jnp.zeros((ROWS, LANES), jnp.bool_)
        hit_before = jnp.zeros((ROWS, LANES), jnp.bool_)
        for slot in range(slots):
            hit = hit | (at == starts[0, slot])
            hit_before = hit_before | (at - 1 == starts[0, slot])
        mask1 = jnp.where(hit, 0.0, 1.0)
        mask2 = jnp.where(hit | hit_before, 0.0, 1.0)
        first = step == 0
        for group in range(GROUPS):
            cols = slice(group * LANES, (group + 1) * LANES)

            def short(ref, index):
                x = ref[pl.ds(row, ROWS), cols].astype(jnp.float32)
                before = ref[pl.ds(back, ROWS), cols].astype(jnp.float32)
                rim = rim_ref[index, :, cols].astype(jnp.float32)
                before = jnp.where(first, rim, before)
                both = jnp.concatenate([before, x], axis=0)
                lag1 = pltpu.roll(both, 1, 0)[ROWS:]
                lag2 = pltpu.roll(both, 2, 0)[ROWS:]
                base = 3 * index
                summed = taps_ref[base : base + 1, cols] * x
                summed = summed + taps_ref[base + 1 : base + 2, cols] * mask1 * lag1
                summed = summed + taps_ref[base + 2 : base + 3, cols] * mask2 * lag2
                return summed.astype(jnp.bfloat16)

            qs_ref[pl.ds(row, ROWS), cols] = short(q_ref, 0)
            gated = short(k_ref, 1).astype(jnp.float32) * short(v_ref, 2).astype(jnp.float32)
            z_ref[pl.ds(row * GROUPS + group, ROWS, stride=GROUPS), :] = gated
        return carry

    lax.fori_loop(0, tokens // ROWS, short_rows, 0)

    fac_ref[...] = jnp.exp(-rate_ref[...])
    skip = skip_ref[...]

    def advance(step, states):
        states = list(states)
        for inner in range(UNROLL):
            time = step * UNROLL + inner
            spot = pl.ds(pl.multiple_of(time * GROUPS, GROUPS), GROUPS)
            keep = jnp.where(time == cut, 0.0, 1.0)
            x = z_ref[spot, :]
            sums = [skip * x, None]
            for n in range(modes):
                states[n] = (fac_ref[n] * keep) * states[n] + x
                term = res_ref[n] * states[n]
                sums[n % 2] = term if sums[n % 2] is None else sums[n % 2] + term
            z_ref[spot, :] = sums[0] + sums[1]
        return tuple(states)

    zero = jnp.zeros((GROUPS, LANES), jnp.float32)
    states = lax.fori_loop(0, tokens // UNROLL, advance, (zero,) * modes)
    for n in range(modes):
        state_ref[n] = states[n]
    through = jnp.where(cut < tokens, 0.0, 1.0)
    for n in range(modes, state_ref.shape[0]):
        state_ref[n] = zero + through


def scan_kernel(tokens, pieces_ref, rate_ref, out_ref):
    modes = rate_ref.shape[0]
    factor = jnp.exp(-float(tokens) * rate_ref[...])

    def hop(j, running):
        out_ref[j] = running
        piece = pieces_ref[j]
        return factor * piece[modes : modes + 1] * running + piece[:modes]

    lax.fori_loop(0, pieces_ref.shape[0], hop, jnp.zeros(rate_ref.shape, jnp.float32))


def finish_kernel(starts, flags, qs_ref, z_ref, enter_ref, rate_ref, res_ref, out_ref, fac_ref,
                  y_ref):
    tokens = qs_ref.shape[0]
    modes = rate_ref.shape[0]
    cut = cut_of(starts, flags, tokens)
    fac_ref[...] = jnp.exp(-rate_ref[...])

    def advance(step, weights):
        weights = list(weights)
        for inner in range(UNROLL):
            time = step * UNROLL + inner
            spot = pl.ds(pl.multiple_of(time * GROUPS, GROUPS), GROUPS)
            alive = jnp.where(time < cut, 1.0, 0.0)
            sums = [None, None]
            for n in range(modes):
                sums[n % 2] = weights[n] if sums[n % 2] is None else sums[n % 2] + weights[n]
                weights[n] = weights[n] * fac_ref[n]
            y_ref[spot, :] = z_ref[spot, :] + alive * (sums[0] + sums[1])
        return tuple(weights)

    begin = tuple(res_ref[n] * (fac_ref[n] * enter_ref[n]) for n in range(modes))
    lax.fori_loop(0, tokens // UNROLL, advance, begin)

    def mix_rows(step, carry):
        row = pl.multiple_of(step * ROWS, ROWS)
        for group in range(GROUPS):
            cols = slice(group * LANES, (group + 1) * LANES)
            y = y_ref[pl.ds(row * GROUPS + group, ROWS, stride=GROUPS), :]
            q = qs_ref[pl.ds(row, ROWS), cols].astype(jnp.float32)
            out_ref[pl.ds(row, ROWS), cols] = (q * y).astype(jnp.bfloat16)
        return carry

    lax.fori_loop(0, tokens // ROWS, mix_rows, 0)


def local(q_feat, k_feat, v_feat, short_taps, decay_rate, residue, skip_gain, out_weight,
          doc_starts, reset_flags):
    tokens, channels = q_feat.shape
    modes = decay_rate.shape[0]
    kinds, taps = short_taps.shape[:2]
    n = lax.axis_size("seq")
    me = lax.axis_index("seq")
    tiles = channels // TILE
    heads = modes + 8

    weight = lax.all_gather(out_weight, "seq", axis=0, tiled=True)

    last_is_start = jnp.any(doc_starts[0] == tokens - 1)
    scale = jnp.stack([jnp.where(last_is_start, 0.0, 1.0), jnp.float32(1.0)]).astype(jnp.bfloat16)
    tails = jnp.stack([x[tokens - (taps - 1) :] for x in (q_feat, k_feat, v_feat)])
    tails = tails * scale[None, :, None]
    arrived = lax.ppermute(tails, "seq", [(i, i + 1) for i in range(n - 1)])
    rim = jnp.pad(arrived, ((0, 0), (ROWS - (taps - 1), 0), (0, 0)))

    rates = decay_rate.reshape(modes, channels // LANES, LANES)
    residues = residue.reshape(modes, channels // LANES, LANES)
    skips = skip_gain.reshape(channels // LANES, LANES)

    smem = pl.BlockSpec(memory_space=pltpu.SMEM)
    wide = pl.BlockSpec((tokens, TILE), lambda i: (0, i))
    deep = pl.BlockSpec((modes, GROUPS, LANES), lambda i: (0, i, 0))
    flat = pl.BlockSpec((None, tokens * GROUPS, LANES), lambda i: (i, 0, 0))
    f32 = jnp.float32
    qs, z, state = pl.pallas_call(
        local_kernel,
        grid=(tiles,),
        in_specs=[
            smem, smem, wide, wide, wide,
            pl.BlockSpec((kinds, ROWS, TILE), lambda i: (0, 0, i)),
            pl.BlockSpec((kinds * taps, TILE), lambda i: (0, i)),
            deep, deep,
            pl.BlockSpec((GROUPS, LANES), lambda i: (i, 0)),
        ],
        out_specs=[wide, flat, pl.BlockSpec((heads, GROUPS, LANES), lambda i: (0, i, 0))],
        out_shape=[
            jax.ShapeDtypeStruct((tokens, channels), jnp.bfloat16),
            jax.ShapeDtypeStruct((tiles, tokens * GROUPS, LANES), f32),
            jax.ShapeDtypeStruct((heads, channels // LANES, LANES), f32),
        ],
        scratch_shapes=[pltpu.VMEM((modes, GROUPS, LANES), f32)],
        cost_estimate=pl.CostEstimate(
            flops=tokens * channels * 80, bytes_accessed=tokens * channels * 12, transcendentals=0
        ),
        name="local_filter",
    )(doc_starts, reset_flags, q_feat, k_feat, v_feat, rim,
      short_taps.reshape(kinds * taps, channels), rates, residues, skips)

    part = channels // n
    sent = state.reshape(heads, n, part).transpose(1, 0, 2)
    pieces = lax.all_to_all(sent, "seq", 0, 0)
    my_rates = lax.dynamic_slice_in_dim(decay_rate, me * part, part, 1)
    chained = pl.pallas_call(
        functools.partial(scan_kernel, tokens),
        out_shape=jax.ShapeDtypeStruct((n, modes, part), f32),
        name="chain_states",
    )(pieces, my_rates)
    entering = lax.all_to_all(chained, "seq", 0, 0)
    entering = entering.transpose(1, 0, 2).reshape(modes, channels // LANES, LANES)

    mixed = pl.pallas_call(
        finish_kernel,
        grid=(tiles,),
        in_specs=[smem, smem, wide, flat, deep, deep, deep],
        out_specs=wide,
        out_shape=jax.ShapeDtypeStruct((tokens, channels), jnp.bfloat16),
        scratch_shapes=[
            pltpu.VMEM((modes, GROUPS, LANES), f32),
            pltpu.VMEM((tokens * GROUPS, LANES), f32),
        ],
        cost_estimate=pl.CostEstimate(
            flops=tokens * channels * 40, bytes_accessed=tokens * channels * 8, transcendentals=0
        ),
        name="finish_filter",
    )(doc_starts, reset_flags, qs, z, entering, rates, residues)

    projected = lax.dot_general(
        mixed, weight, (((1,), (1,)), ((), ())), preferred_element_type=f32
    ).astype(jnp.bfloat16)
    return lax.psum_scatter(projected, "ch", scatter_dimension=1, tiled=True)


def solution(mesh):
    placed = (
        P("seq", "ch"), P("seq", "ch"), P("seq", "ch"), P(None, None, "ch"), P(None, "ch"),
        P(None, "ch"), P("ch"), P("seq", "ch"), P("seq", None), P("seq", None),
    )
    return jax.shard_map(
        local, mesh=mesh, in_specs=placed, out_specs=P("seq", "ch"), check_vma=False
    )
```

time: 599 us -> 242 us (0.40)
  other arithmetic: 167 us -> 1.48 us
  local copies, waits for them, and re-layouts: 144 us -> 11.6 us
  matrix products: 124 us -> 16.9 us
  Pallas kernels: 0 us -> 33.4 us
  blocking collectives: 0 us -> 24.1 us
  waiting for transfers between devices: 139 us -> 130 us
  starting transfers between devices: 3.11 us -> 9.76 us
    dot_general x6 -> x1, matrix products: 124 us -> 16.9 us  [local(): lax.dot_general(mixed, weight, (((1,), (1,)), ((), ())), preferred_elemen...]
    mul x9 -> x1, other arithmetic: 64.9 us -> 0.11 us  [local(): tails = tails * scale[None, :, None]]
    rev x2 -> x0, local copies, waits for them, and re-layouts: 56.6 us -> none  [local(): reversed_powers = powers[:, BLOCK - 1::-1]]
    select_n x31 -> x0, other arithmetic: 39 us -> none  [hop(): jnp.where(position < mine, new, old)]
    dot_general x3 -> x0, other arithmetic: 34.4 us -> none  [the longest x1 15.5 us: local(): jnp.einsum('njc,nc->jc', powers[:, :BLOCK], residue, precision=highest)]
    mul x2 -> x0, local copies, waits for them, and re-layouts: 33.6 us -> none  [the longest x1 33.6 us: local(): weighted = residue[:, None, :] * powers[:, 1:]]
    pallas_call x0 -> x3, Pallas kernels: none -> 33.4 us  [the longest x1 22.4 us: local(): pl.pallas_call(local_kernel, grid=(tiles,), in_specs=[smem, smem, wide, w...]
    all_gather x3 -> x1, waiting for transfers between devices: 138 us -> 109 us  [local(): weight = lax.all_gather(out_weight, 'seq', axis=0, tiled=True)]
  transfers between devices with their start and end apart: 4 -> 3, of which waited for: 2 -> 2; matrix products, arithmetic and copies ran while one was open for 53% -> 5% of each run, Pallas kernels for 0% -> 14%
where the time goes in v1:
time: 242 us; the launch traced here: 241 us
  waiting for transfers between devices  130 us (54%)
  Pallas kernels  33.4 us (14%)
  blocking collectives  24.1 us (10%)
  matrix products  16.9 us (7%)
  between operations  14.1 us (6%)
  local copies, waits for them, and re-layouts  11.6 us (5%)
  starting transfers between devices  9.76 us (4%)
    all_gather x1, waiting for transfers between devices, local(): weight = lax.all_gather(out_weight, 'seq', axis=0, tiled=True)  109 us
    all_to_all x1, blocking collectives, local(): entering = lax.all_to_all(chained, 'seq', 0, 0)  24.1 us
    pallas_call x1, Pallas kernels, local(): pl.pallas_call(local_kernel, grid=(tiles,), in_specs=[smem, smem, wide, w...  22.4 us
    all_to_all x1, waiting for transfers between devices, local(): pieces = lax.all_to_all(sent, 'seq', 0, 0)  19.7 us
    dot_general x1, matrix products, local(): lax.dot_general(mixed, weight, (((1,), (1,)), ((), ())), preferred_elemen...  16.9 us
    pallas_call x1, Pallas kernels, local(): pl.pallas_call(finish_kernel, grid=(tiles,), in_specs=[smem, smem, wide,...  9.07 us
    all_to_all x1, starting transfers between devices, local(): pieces = lax.all_to_all(sent, 'seq', 0, 0)  7.36 us
  transfers between devices with their start and end apart: 3, of which 2 were waited for; matrix products, arithmetic and copies ran while one was open for 5% of the time, Pallas kernels for 14%

profile of v1, /device:TPU:0, one launch (start us, length us, event | category | flops | bytes accessed | tf_op | source)
XLA Modules:
  0.0 241.1 jit_solution(15947912545685952483)
XLA Ops:
  6.5 0.0 copy-start.1
  6.5 0.0 all-gather.2.cloned.1.call-start
  6.5 0.7 all-gather.2.cloned.1.call-update
  7.3 1.3 compare_reduce_fusion
  9.2 0.1 pad_maximum_fusion
  9.3 0.9 slice_bitcast_fusion.2
  10.2 0.9 slice_bitcast_fusion
  11.1 0.1 maximum_multiply_fusion
  11.2 2.4 collective-permute-start
  13.6 1.7 copy.16
  15.3 1.7 copy.15
  17.0 0.0 copy-done.1
  17.0 0.8 reshape.30.taps_ref
  17.8 0.0 collective-permute-done
  17.8 0.8 pad.4.rim_ref
  18.6 22.4 %local_filter.1 = (bf16[256,4096]{1,0:T(8,128)(2,1)}, f32[4,2048,128]{2,1,0:T(8,128)}, f32[24,32,128]{2,1,0:T(8,128)}) custom-call(s32[1,4]{1,0:T(1,128)} %starts.3, s32[1,4]{1,0:T(1,128)} %flags.3, bf16[256,4096]{1,0:T(8,128)(2,1)} %q_ref.1, bf16[256,4096]{1,0:T(8,128)(2,1)} %k_ref.1, bf16[256,4096]{1,0:T(8,128)(2,1)} %v_ref.1, ...), custom_call_target="tpu_custom_call" | custom-call | flops 83886080 | bytes 12582912 | tf_op jit(solution)/shard_map/local_filter/pallas_call | solution.py:169
  41.1 2.0 copy.19
  43.0 7.4 %all-to-all-start = ((f32[32,24,128]{2,1,0:T(8,128)}), f32[32,24,128]{2,1,0:T(8,128)S(1)}, u32[]{:S(2)}, u32[]{:S(2)}) async-start(f32[32,24,128]{2,1,0:T(8,128)} %bitcast.18), calls=%async_computation | async-start | bytes 786432 | tf_op jit(solution)/shard_map/all_to_all | solution.py:195
  50.4 1.3 constant_dynamic-slice_fusion.rate_ref
  51.7 19.7 %all-to-all-done.pieces_ref = f32[32,24,128]{2,1,0:T(8,128)S(1)} async-done(((f32[32,24,128]{2,1,0:T(8,128)}), f32[32,24,128]{2,1,0:T(8,128)S(1)}, u32[]{:S(2)}, u32[]{:S(2)}) %all-to-all-start) | async-done | bytes 393248 | tf_op jit(solution)/shard_map/all_to_all | solution.py:195
  71.5 0.0 copy-start
  71.5 0.8 copy-done
  72.2 1.9 chain_states.1
  74.1 24.1 %all_to_all.10 = f32[32,16,128]{2,1,0:T(8,128)S(1)} all-to-all(f32[32,16,128]{2,1,0:T(8,128)} %chain_states.1), channel_id=1, replica_groups=mesh['seq'=32,'ch'=1] {'seq'}, dimensions={0} | all-to-all | bytes 524288 | tf_op jit(solution)/shard_map/all_to_all | solution.py:202
  98.2 0.8 copy.20
  99.0 9.1 %finish_filter.1 = bf16[256,4096]{1,0:T(8,128)(2,1)} custom-call(s32[1,4]{1,0:T(1,128)} %starts.3, s32[1,4]{1,0:T(1,128)} %flags.3, bf16[256,4096]{1,0:T(8,128)(2,1)} %get-tuple-element.8.qs_ref, f32[4,2048,128]{2,1,0:T(8,128)} %get-tuple-element.9.z_ref, f32[16,32,128]{2,1,0:T(8,128)} %bitcast.24, f32[16,32,128]{2,1,0:T(8,128)} %bitcast.23, ...), custom_call_target="tpu_custom_call" | custom-call | flops 41943040 | bytes 8388608 | tf_op jit(solution)/shard_map/finish_filter/pallas_call | solution.py:205
  108.1 109.3 %all-gather.2.cloned.1.call-done = bf16[4096,4096]{1,0:T(8,128)(2,1)} async-done(((bf16[128,4096]{1,0:T(8,128)(2,1)}), bf16[4096,4096]{1,0:T(8,128)(2,1)}) %all-gather.2.cloned.1.call-update) | async-done | bytes 33554448 | tf_op jit(solution)/shard_map/all_gather | solution.py:151
  217.4 16.9 %convolution_convert_fusion = bf16[256,4096]{1,0:T(8,128)(2,1)} fusion(bf16[256,4096]{1,0:T(8,128)(2,1)} %finish_filter.1, bf16[4096,4096]{1,0:T(8,128)(2,1)} %all-gather.2.cloned.1.call-done), kind=kOutput, calls=%fused_computation | convolution fusion | flops 8590983168 | bytes 37748736 | tf_op jit(solution)/shard_map/dot_general | solution.py:221
Async XLA Ops:
  6.5 10.5 %copy-start.1 = (f32[3,3,4096]{2,1,0:T(4,128)S(1)}, f32[3,3,4096]{2,1,0:T(4,128)}, u32[]{:S(2)}) copy-start(f32[3,3,4096]{2,1,0:T(4,128)} %param.13) | copy-start | bytes 442372
  6.5 210.9 %all-gather.2.cloned.1.call-start = ((), (), s32[]{:S(2)}) async-start(), calls=%async_computation.2 | async-start | bytes 34603008 | tf_op jit(solution)/shard_map/all_gather | solution.py:151
  11.2 6.6 %collective-permute-start = (bf16[3,2,4096]{2,1,0:T(2,128)(2,1)S(1)}, bf16[3,2,4096]{2,1,0:T(2,128)(2,1)S(1)}, u32[]{:S(2)}, u32[]{:S(2)}) collective-permute-start(bf16[3,2,4096]{2,1,0:T(2,128)(2,1)S(1)} %maximum_multiply_fusion), channel_id=1, source_target_pairs={{0,1},{1,2},{2,3},{3,4},{4,5},{5,6},{6,7},{7,8},{8,9},{9,10},{10,1... | collective-permute-start | bytes 147464 | tf_op jit(solution)/shard_map/ppermute | solution.py:157
  43.0 28.4 %all-to-all-start = ((f32[32,24,128]{2,1,0:T(8,128)}), f32[32,24,128]{2,1,0:T(8,128)S(1)}, u32[]{:S(2)}, u32[]{:S(2)}) async-start(f32[32,24,128]{2,1,0:T(8,128)} %bitcast.18), calls=%async_computation | async-start | bytes 786432 | tf_op jit(solution)/shard_map/all_to_all | solution.py:195
  71.5 0.8 copy-start
Sparse Core Ops, SparseCore 0:
  10.2 207.1 all-gather.1

commit v2 on v1

--- a/solution.py
+++ b/solution.py
@@ -12,6 +12,7 @@
 TILE = LANES * GROUPS
 ROWS = 16
 UNROLL = 8
+SHARE = 8
 
 
 def cut_of(starts, flags, tokens):
@@ -138,6 +139,18 @@
     lax.fori_loop(0, tokens // ROWS, mix_rows, 0)
 
 
+def doubling(block, order, n):
+    me = lax.axis_index("seq")
+    held = block[None]
+    for bit in order:
+        other = lax.ppermute(held, "seq", [(i, i ^ (1 << bit)) for i in range(n)])
+        upper = lax.rem(lax.div(me, 1 << bit), 2) == 1
+        held = jnp.where(
+            upper, jnp.concatenate([other, held]), jnp.concatenate([held, other])
+        )
+    return held
+
+
 def local(q_feat, k_feat, v_feat, short_taps, decay_rate, residue, skip_gain, out_weight,
           doc_starts, reset_flags):
     tokens, channels = q_feat.shape
@@ -148,7 +161,16 @@
     tiles = channels // TILE
     heads = modes + 8
 
-    weight = lax.all_gather(out_weight, "seq", axis=0, tiled=True)
+    bits = n.bit_length() - 1
+    share = channels // SHARE if n == 1 << bits and bits >= 3 else 0
+    high = tuple(range(bits - 1, 2, -1))
+    orders = (high + (1, 2, 0), high + (2, 1, 0))
+    doubled = [
+        doubling(out_weight[:, i * share : (i + 1) * share], order, n)
+        for i, order in enumerate(orders)
+        if share
+    ]
+    weight = lax.all_gather(out_weight[:, 2 * share :], "seq", axis=0, tiled=True)
 
     last_is_start = jnp.any(doc_starts[0] == tokens - 1)
     scale = jnp.stack([jnp.where(last_is_start, 0.0, 1.0), jnp.float32(1.0)]).astype(jnp.bfloat16)
@@ -218,9 +240,21 @@
         name="finish_filter",
     )(doc_starts, reset_flags, qs, z, entering, rates, residues)
 
-    projected = lax.dot_general(
-        mixed, weight, (((1,), (1,)), ((), ())), preferred_element_type=f32
-    ).astype(jnp.bfloat16)
+    def project(columns, rows):
+        return lax.dot_general(
+            columns, rows, (((1,), (1,)), ((), ())), preferred_element_type=f32
+        )
+
+    early = jnp.zeros((), f32)
+    features = out_weight.shape[0]
+    for i, (order, rows) in enumerate(zip(orders, doubled)):
+        term = project(mixed[:, i * share : (i + 1) * share], rows.reshape(n * features, share))
+        term = term.reshape((tokens,) + (2,) * bits + (features,))
+        foremost = order[::-1]
+        axes = tuple(1 + foremost.index(bit) for bit in range(bits - 1, -1, -1))
+        term = term.transpose((0,) + axes + (bits + 1,)).reshape(tokens, n * features)
+        early = early + term
+    projected = (project(mixed[:, 2 * share :], weight) + early).astype(jnp.bfloat16)
     return lax.psum_scatter(projected, "ch", scatter_dimension=1, tiled=True)
 
 

time: 242 us -> 257 us (1.062)
  blocking collectives: 24.1 us -> 0 us
  starting transfers between devices: 9.76 us -> 27.2 us
  local copies, waits for them, and re-layouts: 11.6 us -> 25.9 us
  other arithmetic: 1.48 us -> 11.8 us
  waiting for transfers between devices: 130 us -> 125 us
    all_gather x1, waiting for transfers between devices: 109 us -> 0.01 us  [local(): lax.all_gather(out_weight[:, 2 * share:], 'seq', axis=0, tiled=True)]
    ppermute x0 -> x10, waiting for transfers between devices: none -> 84.8 us  [doubling(): other = lax.ppermute(held, 'seq', [(i, i ^ 1 << bit) for i in range(n)])]
    all_to_all x1 -> x0, blocking collectives: 24.1 us -> none  [local(): entering = lax.all_to_all(chained, 'seq', 0, 0)]
    all_to_all x0 -> x1, waiting for transfers between devices: none -> 16.6 us  [local(): entering = lax.all_to_all(chained, 'seq', 0, 0)]
    ppermute x0 -> x10, starting transfers between devices: none -> 15.1 us  [doubling(): other = lax.ppermute(held, 'seq', [(i, i ^ 1 << bit) for i in range(n)])]
    add x0 -> x2, local copies, waits for them, and re-layouts: none -> 13.8 us  [local(): early = early + term]
    select_n x0 -> x10, other arithmetic: none -> 10.9 us  [doubling(): jnp.where(upper, jnp.concatenate([other, held]), jnp.concatenate([held, o...]
    all_to_all x1, waiting for transfers between devices: 19.7 us -> 23.2 us  [local(): pieces = lax.all_to_all(sent, 'seq', 0, 0)]
  transfers between devices with their start and end apart: 3 -> 14, of which waited for: 2 -> 9; matrix products, arithmetic and copies ran while one was open for 5% -> 15% of each run, Pallas kernels for 14% -> 13%
where the time goes in v2:
time: 257 us; the launch traced here: 256 us
  waiting for transfers between devices  125 us (49%)
  Pallas kernels  33.5 us (13%)
  starting transfers between devices  27.2 us (11%)
  local copies, waits for them, and re-layouts  25.9 us (10%)
  matrix products  18.3 us (7%)
  between operations  14.3 us (6%)
  other arithmetic  11.8 us (5%)
    ppermute x10, waiting for transfers between devices, doubling(): other = lax.ppermute(held, 'seq', [(i, i ^ 1 << bit) for i in range(n)])  84.8 us
    all_to_all x1, waiting for transfers between devices, local(): pieces = lax.all_to_all(sent, 'seq', 0, 0)  23.2 us
    pallas_call x1, Pallas kernels, local(): pl.pallas_call(local_kernel, grid=(tiles,), in_specs=[smem, smem, wide, w...  22.5 us
    dot_general x3, matrix products, project(): lax.dot_general(columns, rows, (((1,), (1,)), ((), ())), preferred_elemen...  18.3 us
    all_to_all x1, waiting for transfers between devices, local(): entering = lax.all_to_all(chained, 'seq', 0, 0)  16.6 us
    ppermute x10, starting transfers between devices, doubling(): other = lax.ppermute(held, 'seq', [(i, i ^ 1 << bit) for i in range(n)])  15.1 us
    add x2, local copies, waits for them, and re-layouts, local(): early = early + term  13.8 us
    select_n x10, other arithmetic, doubling(): jnp.where(upper, jnp.concatenate([other, held]), jnp.concatenate([held, o...  10.9 us
  transfers between devices with their start and end apart: 14, of which 9 were waited for; matrix products, arithmetic and copies ran while one was open for 15% of the time, Pallas kernels for 13%

profile of v2, /device:TPU:0, one launch (start us, length us, event | category | flops | bytes accessed | tf_op | source)
XLA Modules:
  0.0 256.0 jit_solution(14557818719733302635)
XLA Ops:
  6.5 2.1 slice.31
  8.7 1.0 slice_bitcast_fusion.4
  9.6 4.1 %collective-permute-start.6 = (bf16[1,128,512]{2,1,0:T(8,128)(2,1)S(1)}, bf16[1,128,512]{2,1,0:T(8,128)(2,1)S(1)}, u32[]{:S(2)}, u32[]{:S(2)}) collective-permute-start(bf16[1,128,512]{2,1,0:T(8,128)(2,1)S(1)} %get-tuple-element.11), channel_id=1, source_target_pairs={{0,16},{1,17},{2,18},{3,19},{4,20},{5,21},{6,22},{7,23},{8,24},{9,... | collective-permute-start | bytes 393224 | tf_op jit(solution)/shard_map/ppermute | solution.py:146
  13.9 9.9 %collective-permute-done.6 = bf16[1,128,512]{2,1,0:T(8,128)(2,1)S(1)} collective-permute-done((bf16[1,128,512]{2,1,0:T(8,128)(2,1)S(1)}, bf16[1,128,512]{2,1,0:T(8,128)(2,1)S(1)}, u32[]{:S(2)}, u32[]{:S(2)}) %collective-permute-start.6) | collective-permute-done | bytes 131104 | tf_op jit(solution)/shard_map/ppermute | solution.py:146
  23.9 1.9 collective-permute-done.1
  25.8 4.8 %collective-permute-start.2 = (bf16[2,128,512]{2,1,0:T(8,128)(2,1)S(1)}, bf16[2,128,512]{2,1,0:T(8,128)(2,1)S(1)}, u32[]{:S(2)}, u32[]{:S(2)}) collective-permute-start(bf16[2,128,512]{2,1,0:T(8,128)(2,1)S(1)} %maximum_select_fusion.8), channel_id=1, source_target_pairs={{0,8},{1,9},{2,10},{3,11},{4,12},{5,13},{6,14},{7,15},{8,0},{9,1},... | collective-permute-start | bytes 786440 | tf_op jit(solution)/shard_map/ppermute | solution.py:146
  30.6 13.7 %collective-permute-done.7 = bf16[2,128,512]{2,1,0:T(8,128)(2,1)S(1)} collective-permute-done((bf16[2,128,512]{2,1,0:T(8,128)(2,1)S(1)}, bf16[2,128,512]{2,1,0:T(8,128)(2,1)S(1)}, u32[]{:S(2)}, u32[]{:S(2)}) %collective-permute-start.7) | collective-permute-done | bytes 262176 | tf_op jit(solution)/shard_map/ppermute | solution.py:146
  44.4 1.7 collective-permute-start.8
  46.1 7.7 %collective-permute-done.2 = bf16[2,128,512]{2,1,0:T(8,128)(2,1)S(1)} collective-permute-done((bf16[2,128,512]{2,1,0:T(8,128)(2,1)S(1)}, bf16[2,128,512]{2,1,0:T(8,128)(2,1)S(1)}, u32[]{:S(2)}, u32[]{:S(2)}) %collective-permute-start.2) | collective-permute-done | bytes 262176 | tf_op jit(solution)/shard_map/ppermute | solution.py:146
  53.9 1.6 collective-permute-start.3
  55.5 0.9 slice_bitcast_fusion.6
  58.6 18.2 %collective-permute-done.3 = bf16[4,128,512]{2,1,0:T(8,128)(2,1)S(1)} collective-permute-done((bf16[4,128,512]{2,1,0:T(8,128)(2,1)S(1)}, bf16[4,128,512]{2,1,0:T(8,128)(2,1)S(1)}, u32[]{:S(2)}, u32[]{:S(2)}) %collective-permute-start.3) | collective-permute-done | bytes 524320 | tf_op jit(solution)/shard_map/ppermute | solution.py:146
  77.0 1.4 collective-permute-start.4
  79.3 33.3 %collective-permute-done.9 = bf16[8,128,512]{2,1,0:T(8,128)(2,1)} collective-permute-done((bf16[8,128,512]{2,1,0:T(8,128)(2,1)S(1)}, bf16[8,128,512]{2,1,0:T(8,128)(2,1)}, u32[]{:S(2)}, u32[]{:S(2)}) %collective-permute-start.9) | collective-permute-done | bytes 1048608 | tf_op jit(solution)/shard_map/ppermute | solution.py:146
  112.7 2.0 maximum_select_fusion.3
  114.8 1.6 maximum_select_fusion.2
  117.1 1.9 collective-permute-start
  122.5 22.5 %local_filter.1 = (bf16[256,4096]{1,0:T(8,128)(2,1)}, f32[4,2048,128]{2,1,0:T(8,128)}, f32[24,32,128]{2,1,0:T(8,128)}) custom-call(s32[1,4]{1,0:T(1,128)} %starts.3, s32[1,4]{1,0:T(1,128)} %flags.3, bf16[256,4096]{1,0:T(8,128)(2,1)} %q_ref.1, bf16[256,4096]{1,0:T(8,128)(2,1)} %k_ref.1, bf16[256,4096]{1,0:T(8,128)(2,1)} %v_ref.1, ...), custom_call_target="tpu_custom_call" | custom-call | flops 83886080 | bytes 12582912 | tf_op jit(solution)/shard_map/local_filter/pallas_call | solution.py:191
  145.0 2.0 copy.31
  147.0 7.3 %all-to-all-start = ((f32[32,24,128]{2,1,0:T(8,128)}), f32[32,24,128]{2,1,0:T(8,128)S(1)}, u32[]{:S(2)}, u32[]{:S(2)}) async-start(f32[32,24,128]{2,1,0:T(8,128)} %bitcast.38), calls=%async_computation | async-start | bytes 786432 | tf_op jit(solution)/shard_map/all_to_all | solution.py:217
  155.0 23.2 %all-to-all-done.pieces_ref = f32[32,24,128]{2,1,0:T(8,128)S(1)} async-done(((f32[32,24,128]{2,1,0:T(8,128)}), f32[32,24,128]{2,1,0:T(8,128)S(1)}, u32[]{:S(2)}, u32[]{:S(2)}) %all-to-all-start) | async-done | bytes 393248 | tf_op jit(solution)/shard_map/all_to_all | solution.py:217
  178.9 1.9 chain_states.1
  180.9 2.8 %all-to-all-start.1 = ((f32[32,16,128]{2,1,0:T(8,128)}), f32[32,16,128]{2,1,0:T(8,128)S(1)}, u32[]{:S(2)}, u32[]{:S(2)}) async-start(f32[32,16,128]{2,1,0:T(8,128)} %chain_states.1), calls=%async_computation.1 | async-start | bytes 524288 | tf_op jit(solution)/shard_map/all_to_all | solution.py:224
  183.7 16.6 %all-to-all-done.1 = f32[32,16,128]{2,1,0:T(8,128)S(1)} async-done(((f32[32,16,128]{2,1,0:T(8,128)}), f32[32,16,128]{2,1,0:T(8,128)S(1)}, u32[]{:S(2)}, u32[]{:S(2)}) %all-to-all-start.1) | async-done | bytes 262176 | tf_op jit(solution)/shard_map/all_to_all | solution.py:224
  201.1 9.1 %finish_filter.1 = bf16[256,4096]{1,0:T(8,128)(2,1)} custom-call(s32[1,4]{1,0:T(1,128)} %starts.3, s32[1,4]{1,0:T(1,128)} %flags.3, bf16[256,4096]{1,0:T(8,128)(2,1)} %get-tuple-element.8.qs_ref, f32[4,2048,128]{2,1,0:T(8,128)} %get-tuple-element.9.z_ref, f32[16,32,128]{2,1,0:T(8,128)} %bitcast.46, f32[16,32,128]{2,1,0:T(8,128)} %bitcast.43, ...), custom_call_target="tpu_custom_call" | custom-call | flops 41943040 | bytes 8388608 | tf_op jit(solution)/shard_map/finish_filter/pallas_call | solution.py:227
  210.1 2.7 %maximum_select_fusion.1 = bf16[32,128,512]{2,1,0:T(8,128)(2,1)S(1)} fusion(bf16[16,128,512]{2,1,0:T(8,128)(2,1)S(1)} %maximum_select_fusion.3, bf16[16,128,512]{2,1,0:T(8,128)(2,1)} %collective-permute-done.10, pred[]{:T(512)S(6)} %eq.25), kind=kLoop, calls=%fused_computation.3 | loop fusion | flops 6291456 | bytes 8388609 | tf_op jit(solution)/shard_map/jit(_where)/select_n | solution.py:148
  212.9 4.0 %maximum_select_fusion = bf16[32,128,512]{2,1,0:T(8,128)(2,1)S(1)} fusion(bf16[16,128,512]{2,1,0:T(8,128)(2,1)} %maximum_select_fusion.2, bf16[16,128,512]{2,1,0:T(8,128)(2,1)} %collective-permute-done.5, pred[]{:T(512)S(6)} %eq.25), kind=kLoop, calls=%fused_computation.2 | loop fusion | flops 6291456 | bytes 8388609 | tf_op jit(solution)/shard_map/jit(_where)/select_n | solution.py:148
  217.0 1.3 fusion.6
  218.2 3.3 %bitcast_add_fusion = f32[256,2,2,2,2,2,128]{0,6,1,2,4,3,5:T(8,128)} fusion(f32[256,2,2,2,2,2,128]{0,6,5,4,3,2,1:T(8,128)S(1)} %fusion.6, bf16[2,2,2,2,2,128,512]{6,5,4,3,2,1,0:T(8,128)(2,1)S(1)} %bitcast.40, bf16[256,4096]{1,0:T(8,128)(2,1)S(1)} %copy-done), kind=kOutput, calls=%fused_computation.4 | convolution fusion | flops 1074790400 | bytes 12845056 | tf_op jit(solution)/shard_map/dot_general | solution.py:244
  221.5 7.4 %copy.18 = f32[256,2,2,2,2,2,128]{6,5,4,3,2,1,0:T(2,128)} copy(f32[256,2,2,2,2,2,128]{0,6,1,2,4,3,5:T(8,128)} %bitcast_add_fusion) | data formatting | bytes 8388608 | tf_op jit(solution)/shard_map/add | solution.py:256
  228.9 6.4 %add.17 = f32[256,4096]{1,0:T(8,128)} reshape(f32[256,2,2,2,2,2,128]{6,5,4,3,2,1,0:T(2,128)} %copy.18) | data formatting | bytes 8388608 | tf_op jit(solution)/shard_map/add | solution.py:256
  235.4 13.8 %fusion = bf16[256,4096]{1,0:T(8,128)(2,1)} fusion(f32[256,4096]{1,0:T(8,128)} %add.17, bf16[4096,3072]{1,0:T(8,128)(2,1)} %all-gather.2.cloned.1.call-done, bf16[256,4096]{1,0:T(8,128)(2,1)S(1)} %copy-done), kind=kOutput, calls=%fused_computation.1 | convolution fusion | flops 6444548096 | bytes 33030144 | tf_op jit(solution)/shard_map/dot_general | solution.py:244
  (41 shorter events, 9.3 us)
Async XLA Ops:
  6.5 228.8 %all-gather.2.cloned.1.call-start = ((), (), s32[]{:S(2)}) async-start(), calls=%async_computation.2 | async-start | bytes 25952256 | tf_op jit(solution)/shard_map/all_gather | solution.py:173
  8.6 47.8 %copy-start.5 = (s32[1,4]{1,0:T(1,128)S(1)}, s32[1,4]{1,0:T(1,128)}, u32[]{:S(2)}) copy-start(s32[1,4]{1,0:T(1,128)} %starts.3) | copy-start | bytes 52
  9.6 14.1 %collective-permute-start.6 = (bf16[1,128,512]{2,1,0:T(8,128)(2,1)S(1)}, bf16[1,128,512]{2,1,0:T(8,128)(2,1)S(1)}, u32[]{:S(2)}, u32[]{:S(2)}) collective-permute-start(bf16[1,128,512]{2,1,0:T(8,128)(2,1)S(1)} %get-tuple-element.11), channel_id=1, source_target_pairs={{0,16},{1,17},{2,18},{3,19},{4,20},{5,21},{6,22},{7,23},{8,24},{9,... | collective-permute-start | bytes 393224 | tf_op jit(solution)/shard_map/ppermute | solution.py:146
  13.8 12.0 %collective-permute-start.1 = (bf16[1,128,512]{2,1,0:T(8,128)(2,1)S(1)}, bf16[1,128,512]{2,1,0:T(8,128)(2,1)S(1)}, u32[]{:S(2)}, u32[]{:S(2)}) collective-permute-start(bf16[1,128,512]{2,1,0:T(8,128)(2,1)S(1)} %get-tuple-element.12), channel_id=1, source_target_pairs={{0,16},{1,17},{2,18},{3,19},{4,20},{5,21},{6,22},{7,23},{8,24},{9,... | collective-permute-start | bytes 393224 | tf_op jit(solution)/shard_map/ppermute | solution.py:146
  23.8 20.5 %collective-permute-start.7 = (bf16[2,128,512]{2,1,0:T(8,128)(2,1)S(1)}, bf16[2,128,512]{2,1,0:T(8,128)(2,1)S(1)}, u32[]{:S(2)}, u32[]{:S(2)}) collective-permute-start(bf16[2,128,512]{2,1,0:T(8,128)(2,1)S(1)} %maximum_select_fusion.9), channel_id=1, source_target_pairs={{0,8},{1,9},{2,10},{3,11},{4,12},{5,13},{6,14},{7,15},{8,0},{9,1},... | collective-permute-start | bytes 786440 | tf_op jit(solution)/shard_map/ppermute | solution.py:146
  25.8 28.0 %collective-permute-start.2 = (bf16[2,128,512]{2,1,0:T(8,128)(2,1)S(1)}, bf16[2,128,512]{2,1,0:T(8,128)(2,1)S(1)}, u32[]{:S(2)}, u32[]{:S(2)}) collective-permute-start(bf16[2,128,512]{2,1,0:T(8,128)(2,1)S(1)} %maximum_select_fusion.8), channel_id=1, source_target_pairs={{0,8},{1,9},{2,10},{3,11},{4,12},{5,13},{6,14},{7,15},{8,0},{9,1},... | collective-permute-start | bytes 786440 | tf_op jit(solution)/shard_map/ppermute | solution.py:146
  44.4 13.3 %collective-permute-start.8 = (bf16[4,128,512]{2,1,0:T(8,128)(2,1)S(1)}, bf16[4,128,512]{2,1,0:T(8,128)(2,1)S(1)}, u32[]{:S(2)}, u32[]{:S(2)}) collective-permute-start(bf16[4,128,512]{2,1,0:T(8,128)(2,1)S(1)} %maximum_select_fusion.7), channel_id=1, source_target_pairs={{0,4},{1,5},{2,6},{3,7},{4,0},{5,1},{6,2},{7,3},{8,12},{9,13},{10,... | collective-permute-start | bytes 1572872 | tf_op jit(solution)/shard_map/ppermute | solution.py:146
  53.9 23.0 %collective-permute-start.3 = (bf16[4,128,512]{2,1,0:T(8,128)(2,1)S(1)}, bf16[4,128,512]{2,1,0:T(8,128)(2,1)S(1)}, u32[]{:S(2)}, u32[]{:S(2)}) collective-permute-start(bf16[4,128,512]{2,1,0:T(8,128)(2,1)S(1)} %maximum_select_fusion.6), channel_id=1, source_target_pairs={{0,2},{1,3},{2,0},{3,1},{4,6},{5,7},{6,4},{7,5},{8,10},{9,11},{10,... | collective-permute-start | bytes 1572872 | tf_op jit(solution)/shard_map/ppermute | solution.py:146
  57.9 54.8 %collective-permute-start.9 = (bf16[8,128,512]{2,1,0:T(8,128)(2,1)S(1)}, bf16[8,128,512]{2,1,0:T(8,128)(2,1)}, u32[]{:S(2)}, u32[]{:S(2)}) collective-permute-start(bf16[8,128,512]{2,1,0:T(8,128)(2,1)S(1)} %maximum_select_fusion.5), channel_id=1, source_target_pairs={{0,2},{1,3},{2,0},{3,1},{4,6},{5,7},{6,4},{7,5},{8,10},{9,11},{10,... | collective-permute-start | bytes 3145736 | tf_op jit(solution)/shard_map/ppermute | solution.py:146
  77.0 37.8 %collective-permute-start.4 = (bf16[8,128,512]{2,1,0:T(8,128)(2,1)S(1)}, bf16[8,128,512]{2,1,0:T(8,128)(2,1)S(1)}, u32[]{:S(2)}, u32[]{:S(2)}) collective-permute-start(bf16[8,128,512]{2,1,0:T(8,128)(2,1)S(1)} %maximum_select_fusion.4), channel_id=1, source_target_pairs={{0,4},{1,5},{2,6},{3,7},{4,0},{5,1},{6,2},{7,3},{8,12},{9,13},{10,... | collective-permute-start | bytes 3145736 | tf_op jit(solution)/shard_map/ppermute | solution.py:146
  114.7 4.3 %copy-start.2 = (f32[16,4096]{1,0:T(8,128)S(1)}, f32[16,4096]{1,0:T(8,128)}, u32[]{:S(2)}) copy-start(f32[16,4096]{1,0:T(8,128)} %param.14) | copy-start | bytes 786436
  114.7 5.1 %copy-start.3 = (f32[16,4096]{1,0:T(8,128)S(1)}, f32[16,4096]{1,0:T(8,128)}, u32[]{:S(2)}) copy-start(f32[16,4096]{1,0:T(8,128)} %param.15) | copy-start | bytes 786436
  114.7 5.8 %copy-start.4 = (f32[3,3,4096]{2,1,0:T(4,128)S(1)}, f32[3,3,4096]{2,1,0:T(4,128)}, u32[]{:S(2)}) copy-start(f32[3,3,4096]{2,1,0:T(4,128)} %param.13) | copy-start | bytes 442372
  114.7 95.4 %collective-permute-start.10 = (bf16[16,128,512]{2,1,0:T(8,128)(2,1)S(1)}, bf16[16,128,512]{2,1,0:T(8,128)(2,1)}, u32[]{:S(2)}, u32[]{:S(2)}) collective-permute-start(bf16[16,128,512]{2,1,0:T(8,128)(2,1)S(1)} %maximum_select_fusion.3), channel_id=1, source_target_pairs={{0,1},{1,0},{2,3},{3,2},{4,5},{5,4},{6,7},{7,6},{8,9},{9,8},{10,11... | collective-permute-start | bytes 6291464 | tf_op jit(solution)/shard_map/ppermute | solution.py:146
  116.5 96.4 %collective-permute-start.5 = (bf16[16,128,512]{2,1,0:T(8,128)(2,1)}, bf16[16,128,512]{2,1,0:T(8,128)(2,1)}, u32[]{:S(2)}, u32[]{:S(2)}) collective-permute-start(bf16[16,128,512]{2,1,0:T(8,128)(2,1)} %maximum_select_fusion.2), channel_id=1, source_target_pairs={{0,1},{1,0},{2,3},{3,2},{4,5},{5,4},{6,7},{7,6},{8,9},{9,8},{10,11... | collective-permute-start | bytes 6291464 | tf_op jit(solution)/shard_map/ppermute | solution.py:146
  117.1 4.7 %collective-permute-start = (bf16[3,2,4096]{2,1,0:T(2,128)(2,1)S(1)}, bf16[3,2,4096]{2,1,0:T(2,128)(2,1)S(1)}, u32[]{:S(2)}, u32[]{:S(2)}) collective-permute-start(bf16[3,2,4096]{2,1,0:T(2,128)(2,1)S(1)} %maximum_multiply_fusion), channel_id=1, source_target_pairs={{0,1},{1,2},{2,3},{3,4},{4,5},{5,6},{6,7},{7,8},{8,9},{9,10},{10,1... | collective-permute-start | bytes 147464 | tf_op jit(solution)/shard_map/ppermute | solution.py:179
  147.0 31.2 %all-to-all-start = ((f32[32,24,128]{2,1,0:T(8,128)}), f32[32,24,128]{2,1,0:T(8,128)S(1)}, u32[]{:S(2)}, u32[]{:S(2)}) async-start(f32[32,24,128]{2,1,0:T(8,128)} %bitcast.38), calls=%async_computation | async-start | bytes 786432 | tf_op jit(solution)/shard_map/all_to_all | solution.py:217
  178.2 0.8 copy-start.1
  180.9 19.4 %all-to-all-start.1 = ((f32[32,16,128]{2,1,0:T(8,128)}), f32[32,16,128]{2,1,0:T(8,128)S(1)}, u32[]{:S(2)}, u32[]{:S(2)}) async-start(f32[32,16,128]{2,1,0:T(8,128)} %chain_states.1), calls=%async_computation.1 | async-start | bytes 524288 | tf_op jit(solution)/shard_map/all_to_all | solution.py:224
  212.9 4.1 %copy-start = (bf16[256,4096]{1,0:T(8,128)(2,1)S(1)}, bf16[256,4096]{1,0:T(8,128)(2,1)}, u32[]{:S(2)}) copy-start(bf16[256,4096]{1,0:T(8,128)(2,1)} %finish_filter.1) | copy-start | bytes 6291460
Sparse Core Ops, SparseCore 0:
  10.2 202.4 all-gather.1

commit v3 on v2

--- a/solution.py
+++ b/solution.py
@@ -139,11 +139,13 @@
     lax.fori_loop(0, tokens // ROWS, mix_rows, 0)
 
 
-def doubling(block, order, n):
+def doubling(block, order, n, beside):
     me = lax.axis_index("seq")
     held = block[None]
-    for bit in order:
+    for stage, bit in enumerate(order):
         other = lax.ppermute(held, "seq", [(i, i ^ (1 << bit)) for i in range(n)])
+        if stage < len(beside):
+            other, _ = lax.optimization_barrier((other, beside[stage]))
         upper = lax.rem(lax.div(me, 1 << bit), 2) == 1
         held = jnp.where(
             upper, jnp.concatenate([other, held]), jnp.concatenate([held, other])
@@ -165,11 +167,6 @@
     share = channels // SHARE if n == 1 << bits and bits >= 3 else 0
     high = tuple(range(bits - 1, 2, -1))
     orders = (high + (1, 2, 0), high + (2, 1, 0))
-    doubled = [
-        doubling(out_weight[:, i * share : (i + 1) * share], order, n)
-        for i, order in enumerate(orders)
-        if share
-    ]
     weight = lax.all_gather(out_weight[:, 2 * share :], "seq", axis=0, tiled=True)
 
     last_is_start = jnp.any(doc_starts[0] == tokens - 1)
@@ -240,6 +237,12 @@
         name="finish_filter",
     )(doc_starts, reset_flags, qs, z, entering, rates, residues)
 
+    doubled = [
+        doubling(out_weight[:, i * share : (i + 1) * share], order, n, (qs, pieces, entering, mixed))
+        for i, order in enumerate(orders)
+        if share
+    ]
+
     def project(columns, rows):
         return lax.dot_general(
             columns, rows, (((1,), (1,)), ((), ())), preferred_element_type=f32

time: 257 us -> 247 us (0.961)
  waiting for transfers between devices: 125 us -> 116 us
  other arithmetic: 11.8 us -> 15 us
    ppermute x10, waiting for transfers between devices: 84.8 us -> 116 us  [doubling(): other = lax.ppermute(held, 'seq', [(i, i ^ 1 << bit) for i in range(n)])]
    all_to_all x1, waiting for transfers between devices: 23.2 us -> 0.01 us  [local(): pieces = lax.all_to_all(sent, 'seq', 0, 0)]
    all_to_all x1, waiting for transfers between devices: 16.6 us -> 0.01 us  [local(): entering = lax.all_to_all(chained, 'seq', 0, 0)]
    ppermute x10, starting transfers between devices: 15.1 us -> 10.9 us  [doubling(): other = lax.ppermute(held, 'seq', [(i, i ^ 1 << bit) for i in range(n)])]
    select_n x10, other arithmetic: 10.9 us -> 14.1 us  [doubling(): jnp.where(upper, jnp.concatenate([other, held]), jnp.concatenate([held, o...]
  transfers between devices with their start and end apart: 14 -> 14, of which waited for: 9 -> 8; matrix products, arithmetic and copies ran while one was open for 15% -> 17% of each run, Pallas kernels for 13% -> 14%
where the time goes in v3:
time: 247 us; the launch traced here: 246 us
  waiting for transfers between devices  116 us (47%)
  Pallas kernels  33.3 us (13%)
  local copies, waits for them, and re-layouts  25.3 us (10%)
  starting transfers between devices  24.7 us (10%)
  matrix products  18.3 us (7%)
  other arithmetic  15 us (6%)
  between operations  14.2 us (6%)
    ppermute x10, waiting for transfers between devices, doubling(): other = lax.ppermute(held, 'seq', [(i, i ^ 1 << bit) for i in range(n)])  116 us
    pallas_call x1, Pallas kernels, local(): pl.pallas_call(local_kernel, grid=(tiles,), in_specs=[smem, smem, wide, w...  22.4 us
    dot_general x3, matrix products, project(): lax.dot_general(columns, rows, (((1,), (1,)), ((), ())), preferred_elemen...  18.3 us
    select_n x10, other arithmetic, doubling(): jnp.where(upper, jnp.concatenate([other, held]), jnp.concatenate([held, o...  14.1 us
    add x2, local copies, waits for them, and re-layouts, local(): early = early + term  13.8 us
    ppermute x10, starting transfers between devices, doubling(): other = lax.ppermute(held, 'seq', [(i, i ^ 1 << bit) for i in range(n)])  10.9 us
    pallas_call x1, Pallas kernels, local(): pl.pallas_call(finish_kernel, grid=(tiles,), in_specs=[smem, smem, wide,...  9.04 us
    all_to_all x1, starting transfers between devices, local(): pieces = lax.all_to_all(sent, 'seq', 0, 0)  8.2 us
  transfers between devices with their start and end apart: 14, of which 8 were waited for; matrix products, arithmetic and copies ran while one was open for 17% of the time, Pallas kernels for 14%

profile of v3, /device:TPU:0, one launch (start us, length us, event | category | flops | bytes accessed | tf_op | source)
XLA Modules:
  0.0 246.5 jit_solution(10233579751931021285)
XLA Ops:
  6.6 2.2 slice.31
  12.1 2.4 collective-permute-start
  17.6 22.4 %local_filter.1 = (bf16[256,4096]{1,0:T(8,128)(2,1)}, f32[4,2048,128]{2,1,0:T(8,128)}, f32[24,32,128]{2,1,0:T(8,128)}) custom-call(s32[1,4]{1,0:T(1,128)} %starts.3, s32[1,4]{1,0:T(1,128)} %flags.3, bf16[256,4096]{1,0:T(8,128)(2,1)} %q_ref.1, bf16[256,4096]{1,0:T(8,128)(2,1)} %k_ref.1, bf16[256,4096]{1,0:T(8,128)(2,1)} %v_ref.1, ...), custom_call_target="tpu_custom_call" | custom-call | flops 83886080 | bytes 12582912 | tf_op jit(solution)/shard_map/local_filter/pallas_call | solution.py:188
  40.0 2.0 copy.31
  42.0 8.2 %all-to-all-start = ((f32[32,24,128]{2,1,0:T(8,128)}), f32[32,24,128]{2,1,0:T(8,128)S(1)}, u32[]{:S(2)}, u32[]{:S(2)}) async-start(f32[32,24,128]{2,1,0:T(8,128)} %bitcast.38), calls=%async_computation | async-start | bytes 786432 | tf_op jit(solution)/shard_map/all_to_all | solution.py:214
  51.2 2.7 %collective-permute-start.6 = (bf16[1,128,512]{2,1,0:T(8,128)(2,1)S(1)}, bf16[1,128,512]{2,1,0:T(8,128)(2,1)S(1)}, u32[]{:S(2)}, u32[]{:S(2)}) collective-permute-start(bf16[1,128,512]{2,1,0:T(8,128)(2,1)S(1)} %get-tuple-element.27), channel_id=1, source_target_pairs={{0,16},{1,17},{2,18},{3,19},{4,20},{5,21},{6,22},{7,23},{8,24},{9,... | collective-permute-start | bytes 393224 | tf_op jit(solution)/shard_map/ppermute | solution.py:146
  53.9 34.0 %collective-permute-done.6 = bf16[1,128,512]{2,1,0:T(8,128)(2,1)S(1)} collective-permute-done((bf16[1,128,512]{2,1,0:T(8,128)(2,1)S(1)}, bf16[1,128,512]{2,1,0:T(8,128)(2,1)S(1)}, u32[]{:S(2)}, u32[]{:S(2)}) %collective-permute-start.6) | collective-permute-done | bytes 131104 | tf_op jit(solution)/shard_map/ppermute | solution.py:146
  88.1 1.2 collective-permute-start.1
  89.9 11.2 %collective-permute-done.1 = bf16[1,128,512]{2,1,0:T(8,128)(2,1)S(1)} collective-permute-done((bf16[1,128,512]{2,1,0:T(8,128)(2,1)S(1)}, bf16[1,128,512]{2,1,0:T(8,128)(2,1)S(1)}, u32[]{:S(2)}, u32[]{:S(2)}) %collective-permute-start.1) | collective-permute-done | bytes 131104 | tf_op jit(solution)/shard_map/ppermute | solution.py:146
  101.1 4.0 %collective-permute-done.7 = bf16[2,128,512]{2,1,0:T(8,128)(2,1)S(1)} collective-permute-done((bf16[2,128,512]{2,1,0:T(8,128)(2,1)S(1)}, bf16[2,128,512]{2,1,0:T(8,128)(2,1)S(1)}, u32[]{:S(2)}, u32[]{:S(2)}) %collective-permute-start.7) | collective-permute-done | bytes 262176 | tf_op jit(solution)/shard_map/ppermute | solution.py:146
  105.2 1.5 collective-permute-start.8
  106.7 1.9 chain_states.1
  108.6 3.2 %all-to-all-start.1 = ((f32[32,16,128]{2,1,0:T(8,128)}), f32[32,16,128]{2,1,0:T(8,128)S(1)}, u32[]{:S(2)}, u32[]{:S(2)}) async-start(f32[32,16,128]{2,1,0:T(8,128)} %chain_states.1), calls=%async_computation.1 | async-start | bytes 524288 | tf_op jit(solution)/shard_map/all_to_all | solution.py:221
  111.8 1.7 collective-permute-start.2
  113.5 33.7 %collective-permute-done.2 = bf16[2,128,512]{2,1,0:T(8,128)(2,1)S(1)} collective-permute-done((bf16[2,128,512]{2,1,0:T(8,128)(2,1)S(1)}, bf16[2,128,512]{2,1,0:T(8,128)(2,1)S(1)}, u32[]{:S(2)}, u32[]{:S(2)}) %collective-permute-start.2) | collective-permute-done | bytes 262176 | tf_op jit(solution)/shard_map/ppermute | solution.py:146
  147.3 1.5 collective-permute-start.3
  150.4 18.6 %collective-permute-done.3 = bf16[4,128,512]{2,1,0:T(8,128)(2,1)S(1)} collective-permute-done((bf16[4,128,512]{2,1,0:T(8,128)(2,1)S(1)}, bf16[4,128,512]{2,1,0:T(8,128)(2,1)S(1)}, u32[]{:S(2)}, u32[]{:S(2)}) %collective-permute-start.3) | collective-permute-done | bytes 524320 | tf_op jit(solution)/shard_map/ppermute | solution.py:146
  169.0 1.2 maximum_select_fusion.4
  170.2 1.5 collective-permute-start.4
  171.6 9.0 %finish_filter.1 = bf16[256,4096]{1,0:T(8,128)(2,1)} custom-call(s32[1,4]{1,0:T(1,128)} %starts.3, s32[1,4]{1,0:T(1,128)} %flags.3, bf16[256,4096]{1,0:T(8,128)(2,1)} %get-tuple-element.16.qs_ref, f32[4,2048,128]{2,1,0:T(8,128)} %get-tuple-element.17.z_ref, f32[16,32,128]{2,1,0:T(8,128)} %bitcast.46, f32[16,32,128]{2,1,0:T(8,128)} %bitcast.43, ...), custom_call_target="tpu_custom_call" | custom-call | flops 41943040 | bytes 8388608 | tf_op jit(solution)/shard_map/finish_filter/pallas_call | solution.py:224
  180.7 10.6 %collective-permute-done.9 = bf16[8,128,512]{2,1,0:T(8,128)(2,1)} collective-permute-done((bf16[8,128,512]{2,1,0:T(8,128)(2,1)S(1)}, bf16[8,128,512]{2,1,0:T(8,128)(2,1)}, u32[]{:S(2)}, u32[]{:S(2)}) %collective-permute-start.9) | collective-permute-done | bytes 1048608 | tf_op jit(solution)/shard_map/ppermute | solution.py:146
  191.3 2.0 maximum_select_fusion.3
  193.4 1.7 collective-permute-done.4
  195.1 3.9 %maximum_select_fusion.2 = bf16[16,128,512]{2,1,0:T(8,128)(2,1)} fusion(bf16[8,128,512]{2,1,0:T(8,128)(2,1)} %maximum_select_fusion.4, bf16[8,128,512]{2,1,0:T(8,128)(2,1)} %collective-permute-done.4, pred[]{:T(512)S(6)} %eq.26), kind=kLoop, calls=%fused_computation.7 | loop fusion | flops 3145728 | bytes 4194305 | tf_op jit(solution)/shard_map/jit(_where)/select_n | solution.py:150
  199.0 2.7 %maximum_select_fusion.1 = bf16[32,128,512]{2,1,0:T(8,128)(2,1)S(1)} fusion(bf16[16,128,512]{2,1,0:T(8,128)(2,1)S(1)} %maximum_select_fusion.3, bf16[16,128,512]{2,1,0:T(8,128)(2,1)} %collective-permute-done.10, pred[]{:T(512)S(6)} %eq.25), kind=kLoop, calls=%fused_computation.3 | loop fusion | flops 6291456 | bytes 8388609 | tf_op jit(solution)/shard_map/jit(_where)/select_n | solution.py:150
  201.7 1.8 collective-permute-done.5
  203.5 4.0 %maximum_select_fusion = bf16[32,128,512]{2,1,0:T(8,128)(2,1)S(1)} fusion(bf16[16,128,512]{2,1,0:T(8,128)(2,1)} %maximum_select_fusion.2, bf16[16,128,512]{2,1,0:T(8,128)(2,1)} %collective-permute-done.5, pred[]{:T(512)S(6)} %eq.25), kind=kLoop, calls=%fused_computation.2 | loop fusion | flops 6291456 | bytes 8388609 | tf_op jit(solution)/shard_map/jit(_where)/select_n | solution.py:150
  207.5 1.3 fusion.6
  208.7 3.3 %bitcast_add_fusion = f32[256,2,2,2,2,2,128]{0,6,1,2,4,3,5:T(8,128)} fusion(f32[256,2,2,2,2,2,128]{0,6,5,4,3,2,1:T(8,128)S(1)} %fusion.6, bf16[2,2,2,2,2,128,512]{6,5,4,3,2,1,0:T(8,128)(2,1)S(1)} %bitcast.40, bf16[256,4096]{1,0:T(8,128)(2,1)S(1)} %copy-done), kind=kOutput, calls=%fused_computation.4 | convolution fusion | flops 1074790400 | bytes 12845056 | tf_op jit(solution)/shard_map/dot_general | solution.py:247
  212.0 7.4 %copy.18 = f32[256,2,2,2,2,2,128]{6,5,4,3,2,1,0:T(2,128)} copy(f32[256,2,2,2,2,2,128]{0,6,1,2,4,3,5:T(8,128)} %bitcast_add_fusion) | data formatting | bytes 8388608 | tf_op jit(solution)/shard_map/add | solution.py:259
  219.4 6.4 %add.17 = f32[256,4096]{1,0:T(8,128)} reshape(f32[256,2,2,2,2,2,128]{6,5,4,3,2,1,0:T(2,128)} %copy.18) | data formatting | bytes 8388608 | tf_op jit(solution)/shard_map/add | solution.py:259
  225.9 13.8 %fusion = bf16[256,4096]{1,0:T(8,128)(2,1)} fusion(f32[256,4096]{1,0:T(8,128)} %add.17, bf16[4096,3072]{1,0:T(8,128)(2,1)} %all-gather.2.cloned.1.call-done, bf16[256,4096]{1,0:T(8,128)(2,1)S(1)} %copy-done), kind=kOutput, calls=%fused_computation.1 | convolution fusion | flops 6444548096 | bytes 33030144 | tf_op jit(solution)/shard_map/dot_general | solution.py:247
  (41 shorter events, 9.3 us)
Async XLA Ops:
  6.5 2.3 copy-start.5
  6.5 7.9 %copy-start.2 = (f32[16,4096]{1,0:T(8,128)S(1)}, f32[16,4096]{1,0:T(8,128)}, u32[]{:S(2)}) copy-start(f32[16,4096]{1,0:T(8,128)} %param.14) | copy-start | bytes 786436
  6.5 8.7 %copy-start.3 = (f32[16,4096]{1,0:T(8,128)S(1)}, f32[16,4096]{1,0:T(8,128)}, u32[]{:S(2)}) copy-start(f32[16,4096]{1,0:T(8,128)} %param.15) | copy-start | bytes 786436
  6.5 9.5 %copy-start.4 = (f32[3,3,4096]{2,1,0:T(4,128)S(1)}, f32[3,3,4096]{2,1,0:T(4,128)}, u32[]{:S(2)}) copy-start(f32[3,3,4096]{2,1,0:T(4,128)} %param.13) | copy-start | bytes 442372
  6.5 219.3 %all-gather.2.cloned.1.call-start = ((), (), s32[]{:S(2)}) async-start(), calls=%async_computation.2 | async-start | bytes 25952256 | tf_op jit(solution)/shard_map/all_gather | solution.py:170
  12.1 4.7 %collective-permute-start = (bf16[3,2,4096]{2,1,0:T(2,128)(2,1)S(1)}, bf16[3,2,4096]{2,1,0:T(2,128)(2,1)S(1)}, u32[]{:S(2)}, u32[]{:S(2)}) collective-permute-start(bf16[3,2,4096]{2,1,0:T(2,128)(2,1)S(1)} %maximum_multiply_fusion), channel_id=1, source_target_pairs={{0,1},{1,2},{2,3},{3,4},{4,5},{5,6},{6,7},{7,8},{8,9},{9,10},{10,1... | collective-permute-start | bytes 147464 | tf_op jit(solution)/shard_map/ppermute | solution.py:176
  42.0 63.1 %all-to-all-start = ((f32[32,24,128]{2,1,0:T(8,128)}), f32[32,24,128]{2,1,0:T(8,128)S(1)}, u32[]{:S(2)}, u32[]{:S(2)}) async-start(f32[32,24,128]{2,1,0:T(8,128)} %bitcast.38), calls=%async_computation | async-start | bytes 786432 | tf_op jit(solution)/shard_map/all_to_all | solution.py:214
  51.2 36.8 %collective-permute-start.6 = (bf16[1,128,512]{2,1,0:T(8,128)(2,1)S(1)}, bf16[1,128,512]{2,1,0:T(8,128)(2,1)S(1)}, u32[]{:S(2)}, u32[]{:S(2)}) collective-permute-start(bf16[1,128,512]{2,1,0:T(8,128)(2,1)S(1)} %get-tuple-element.27), channel_id=1, source_target_pairs={{0,16},{1,17},{2,18},{3,19},{4,20},{5,21},{6,22},{7,23},{8,24},{9,... | collective-permute-start | bytes 393224 | tf_op jit(solution)/shard_map/ppermute | solution.py:146
  88.0 17.1 %collective-permute-start.7 = (bf16[2,128,512]{2,1,0:T(8,128)(2,1)S(1)}, bf16[2,128,512]{2,1,0:T(8,128)(2,1)S(1)}, u32[]{:S(2)}, u32[]{:S(2)}) collective-permute-start(bf16[2,128,512]{2,1,0:T(8,128)(2,1)S(1)} %maximum_select_fusion.9), channel_id=1, source_target_pairs={{0,8},{1,9},{2,10},{3,11},{4,12},{5,13},{6,14},{7,15},{8,0},{9,1},... | collective-permute-start | bytes 786440 | tf_op jit(solution)/shard_map/ppermute | solution.py:146
  88.1 13.0 %collective-permute-start.1 = (bf16[1,128,512]{2,1,0:T(8,128)(2,1)S(1)}, bf16[1,128,512]{2,1,0:T(8,128)(2,1)S(1)}, u32[]{:S(2)}, u32[]{:S(2)}) collective-permute-start(bf16[1,128,512]{2,1,0:T(8,128)(2,1)S(1)} %get-tuple-element.28), channel_id=1, source_target_pairs={{0,16},{1,17},{2,18},{3,19},{4,20},{5,21},{6,22},{7,23},{8,24},{9,... | collective-permute-start | bytes 393224 | tf_op jit(solution)/shard_map/ppermute | solution.py:146
  105.1 1.6 copy-start.1
  105.2 44.4 %collective-permute-start.8 = (bf16[4,128,512]{2,1,0:T(8,128)(2,1)S(1)}, bf16[4,128,512]{2,1,0:T(8,128)(2,1)S(1)}, u32[]{:S(2)}, u32[]{:S(2)}) collective-permute-start(bf16[4,128,512]{2,1,0:T(8,128)(2,1)S(1)} %maximum_select_fusion.7), channel_id=1, source_target_pairs={{0,4},{1,5},{2,6},{3,7},{4,0},{5,1},{6,2},{7,3},{8,12},{9,13},{10,... | collective-permute-start | bytes 1572872 | tf_op jit(solution)/shard_map/ppermute | solution.py:146
  108.6 40.2 %all-to-all-start.1 = ((f32[32,16,128]{2,1,0:T(8,128)}), f32[32,16,128]{2,1,0:T(8,128)S(1)}, u32[]{:S(2)}, u32[]{:S(2)}) async-start(f32[32,16,128]{2,1,0:T(8,128)} %chain_states.1), calls=%async_computation.1 | async-start | bytes 524288 | tf_op jit(solution)/shard_map/all_to_all | solution.py:221
  111.8 35.3 %collective-permute-start.2 = (bf16[2,128,512]{2,1,0:T(8,128)(2,1)S(1)}, bf16[2,128,512]{2,1,0:T(8,128)(2,1)S(1)}, u32[]{:S(2)}, u32[]{:S(2)}) collective-permute-start(bf16[2,128,512]{2,1,0:T(8,128)(2,1)S(1)} %maximum_select_fusion.8), channel_id=1, source_target_pairs={{0,8},{1,9},{2,10},{3,11},{4,12},{5,13},{6,14},{7,15},{8,0},{9,1},... | collective-permute-start | bytes 786440 | tf_op jit(solution)/shard_map/ppermute | solution.py:146
  147.3 21.8 %collective-permute-start.3 = (bf16[4,128,512]{2,1,0:T(8,128)(2,1)S(1)}, bf16[4,128,512]{2,1,0:T(8,128)(2,1)S(1)}, u32[]{:S(2)}, u32[]{:S(2)}) collective-permute-start(bf16[4,128,512]{2,1,0:T(8,128)(2,1)S(1)} %maximum_select_fusion.6), channel_id=1, source_target_pairs={{0,2},{1,3},{2,0},{3,1},{4,6},{5,7},{6,4},{7,5},{8,10},{9,11},{10,... | collective-permute-start | bytes 1572872 | tf_op jit(solution)/shard_map/ppermute | solution.py:146
  149.7 41.6 %collective-permute-start.9 = (bf16[8,128,512]{2,1,0:T(8,128)(2,1)S(1)}, bf16[8,128,512]{2,1,0:T(8,128)(2,1)}, u32[]{:S(2)}, u32[]{:S(2)}) collective-permute-start(bf16[8,128,512]{2,1,0:T(8,128)(2,1)S(1)} %maximum_select_fusion.5), channel_id=1, source_target_pairs={{0,2},{1,3},{2,0},{3,1},{4,6},{5,7},{6,4},{7,5},{8,10},{9,11},{10,... | collective-permute-start | bytes 3145736 | tf_op jit(solution)/shard_map/ppermute | solution.py:146
  170.2 24.9 %collective-permute-start.4 = (bf16[8,128,512]{2,1,0:T(8,128)(2,1)}, bf16[8,128,512]{2,1,0:T(8,128)(2,1)}, u32[]{:S(2)}, u32[]{:S(2)}) collective-permute-start(bf16[8,128,512]{2,1,0:T(8,128)(2,1)} %maximum_select_fusion.4), channel_id=1, source_target_pairs={{0,4},{1,5},{2,6},{3,7},{4,0},{5,1},{6,2},{7,3},{8,12},{9,13},{10,... | collective-permute-start | bytes 3145736 | tf_op jit(solution)/shard_map/ppermute | solution.py:146
  193.3 5.7 %collective-permute-start.10 = (bf16[16,128,512]{2,1,0:T(8,128)(2,1)S(1)}, bf16[16,128,512]{2,1,0:T(8,128)(2,1)}, u32[]{:S(2)}, u32[]{:S(2)}) collective-permute-start(bf16[16,128,512]{2,1,0:T(8,128)(2,1)S(1)} %maximum_select_fusion.3), channel_id=1, source_target_pairs={{0,1},{1,0},{2,3},{3,2},{4,5},{5,4},{6,7},{7,6},{8,9},{9,8},{10,11... | collective-permute-start | bytes 6291464 | tf_op jit(solution)/shard_map/ppermute | solution.py:146
  199.0 4.5 %collective-permute-start.5 = (bf16[16,128,512]{2,1,0:T(8,128)(2,1)}, bf16[16,128,512]{2,1,0:T(8,128)(2,1)}, u32[]{:S(2)}, u32[]{:S(2)}) collective-permute-start(bf16[16,128,512]{2,1,0:T(8,128)(2,1)} %maximum_select_fusion.2), channel_id=1, source_target_pairs={{0,1},{1,0},{2,3},{3,2},{4,5},{5,4},{6,7},{7,6},{8,9},{9,8},{10,11... | collective-permute-start | bytes 6291464 | tf_op jit(solution)/shard_map/ppermute | solution.py:146
  201.7 5.7 %copy-start = (bf16[256,4096]{1,0:T(8,128)(2,1)S(1)}, bf16[256,4096]{1,0:T(8,128)(2,1)}, u32[]{:S(2)}) copy-start(bf16[256,4096]{1,0:T(8,128)(2,1)} %finish_filter.1) | copy-start | bytes 6291460
Sparse Core Ops, SparseCore 0:
  10.2 186.8 all-gather.1
